TPU v7x, 32 devices: a whole 2x2x4 slice. The times are simulated.
32 devices in a mesh: rows: 8 (over y, x, core), cols: 4 (over z).
Axes of the slice: x: 2, y: 2, z: 4, core: 2. Of those that a mesh axis runs over, the one named last changes fastest.
Arguments:
- images: float32 [4, 56, 28, 512], P(None, 'rows', 'cols')
- cotangent: float32 [4, 56, 28, 512], P(None, 'rows', 'cols'), may hold values from -6 to 6
- rel_index: int32 [49, 49], replicated, may hold values from 0 to 168, as said below
- rel_table: float32 [169, 16], replicated
- qkv_weight: bfloat16 [512, 1536], P(('rows', 'cols')), may hold values from -0.25 to 0.25
- proj_weight: bfloat16 [512, 512], P(('rows', 'cols')), may hold values from -1 to 1
- up_weight: bfloat16 [512, 2048], P(('rows', 'cols')), may hold values from -0.25 to 0.25
- down_weight: bfloat16 [2048, 512], P(('rows', 'cols')), may hold values from -0.125 to 0.125
- norm1_gain: bfloat16 [512], P(('rows', 'cols')), may hold values from 0.5 to 1.5
- norm1_bias: bfloat16 [512], P(('rows', 'cols')), may hold values from -3 to 3
- query_bias: bfloat16 [512], P(('rows', 'cols')), may hold values from -3 to 3
- value_bias: bfloat16 [512], P(('rows', 'cols')), may hold values from -3 to 3
- proj_bias: bfloat16 [512], P(('rows', 'cols')), may hold values from -3 to 3
- norm2_gain: bfloat16 [512], P(('rows', 'cols')), may hold values from 0.5 to 1.5
- norm2_bias: bfloat16 [512], P(('rows', 'cols')), may hold values from -3 to 3
- up_bias: bfloat16 [2048], P(('rows', 'cols')), may hold values from -3 to 3
- down_bias: bfloat16 [512], P(('rows', 'cols')), may hold values from -3 to 3
Outputs:
- block_out: float32 [4, 56, 28, 512], P(None, 'rows', 'cols')
- grad_images: float32 [4, 56, 28, 512], P(None, 'rows', 'cols')
- grad_qkv_weight: float32 [512, 1536], P(('rows', 'cols'))
- grad_proj_weight: float32 [512, 512], P(('rows', 'cols'))
- grad_up_weight: float32 [512, 2048], P(('rows', 'cols'))
- grad_down_weight: float32 [2048, 512], P(('rows', 'cols'))
- grad_norm1_gain: float32 [512], P(('rows', 'cols'))
- grad_norm1_bias: float32 [512], P(('rows', 'cols'))
- grad_query_bias: float32 [512], P(('rows', 'cols'))
- grad_value_bias: float32 [512], P(('rows', 'cols'))
- grad_proj_bias: float32 [512], P(('rows', 'cols'))
- grad_norm2_gain: float32 [512], P(('rows', 'cols'))
- grad_norm2_bias: float32 [512], P(('rows', 'cols'))
- grad_up_bias: float32 [2048], P(('rows', 'cols'))
- grad_down_bias: float32 [512], P(('rows', 'cols'))
- grad_rel_table: float32 [169, 16], replicated
Inputs may be any that keep to these rules, and one draw needn't show every extreme that they name: `rel_index`: every value from 0 to 168 appears.
All inputs are finite; a program needn't handle non-finite values.
Results may differ from a plain program's by a relative error of at most 0.012.
Values may be sent and summed in bfloat16 or wider, within the bound.
A program may use at most 128 MiB of HBM per device.

v0:
```python
import jax
import jax.numpy as jnp
from jax import lax
from jax.sharding import PartitionSpec as P

WIN = 7
SHIFT = 3


norm_eps = 1e-05
root_half = 0.7071067811865476
tau_factor = 0.3989422804014327
big_negative = -1e30


def shifted(array, axis, by):
    length = lax.axis_size(axis)
    return lax.ppermute(array, axis, [(i, (i + by) % length) for i in range(length)])


def as_sent(array):

    def short(part):
        return part.astype(jnp.bfloat16) if part.dtype == jnp.float32 else part

    return jax.tree.map(short, array)


def layer_norm(values, gain_vec, offset):
    mean_val = jnp.mean(values, axis=-1, keepdims=True)
    centred = values - mean_val
    inv_std = lax.rsqrt(jnp.mean(centred * centred, axis=-1, keepdims=True) + norm_eps)
    normed = centred * inv_std
    return (normed * gain_vec + offset, normed, inv_std)


def norm_back(grad_out, normed, inv_std, gain_vec):
    scaled = grad_out * gain_vec
    row_inner = (
        scaled
        - jnp.mean(scaled, axis=-1, keepdims=True)
        - normed * jnp.mean(scaled * normed, axis=-1, keepdims=True)
    )
    return (inv_std * row_inner, jnp.sum(grad_out * normed, axis=0), jnp.sum(grad_out, axis=0))


def dot_plain(former, latter):
    return jnp.dot(former, latter, preferred_element_type=jnp.float32)


def dot_lead(former, latter):
    return lax.dot_general(
        former, latter, (((0,), (0,)), ((), ())), preferred_element_type=jnp.float32
    )


def dot_tail(former, latter):
    return lax.dot_general(
        former, latter, (((1,), (1,)), ((), ())), preferred_element_type=jnp.float32
    )


def band_of(positions, length):
    return (positions >= length - WIN).astype(jnp.int32) + (positions >= length - SHIFT).astype(
        jnp.int32
    )


def roll_in(images, cotangent):
    from_below = shifted((images[:, :SHIFT], cotangent[:, :SHIFT]), "rows", -1)
    tall_tokens = jnp.concatenate([images[:, SHIFT:], from_below[0]], axis=1)
    tall_grads = jnp.concatenate([cotangent[:, SHIFT:], from_below[1]], axis=1)
    beside = shifted((tall_tokens[:, :, :SHIFT], tall_grads[:, :, :SHIFT]), "cols", -1)
    return (
        jnp.concatenate([tall_tokens[:, :, SHIFT:], beside[0]], axis=2),
        jnp.concatenate([tall_grads[:, :, SHIFT:], beside[1]], axis=2),
    )


def roll_out(result, grad_tokens):
    from_above = (
        shifted(result[:, -SHIFT:].astype(jnp.bfloat16), "rows", 1).astype(jnp.float32),
        shifted(grad_tokens[:, -SHIFT:].astype(jnp.bfloat16), "rows", 1).astype(jnp.float32),
    )
    tall_result = jnp.concatenate([from_above[0], result[:, :-SHIFT]], axis=1)
    tall_grads = jnp.concatenate([from_above[1], grad_tokens[:, :-SHIFT]], axis=1)
    beside = (
        shifted(tall_result[:, :, -SHIFT:].astype(jnp.bfloat16), "cols", 1).astype(jnp.float32),
        shifted(as_sent(tall_grads[:, :, -SHIFT:]), "cols", 1),
    )
    return (
        jnp.concatenate([beside[0], tall_result[:, :, :-SHIFT]], axis=2),
        jnp.concatenate([beside[1], tall_grads[:, :, :-SHIFT]], axis=2),
    )


def per_device(
    images,
    cotangent,
    rel_index,
    rel_table,
    qkv_weight,
    proj_weight,
    up_weight,
    down_weight,
    norm1_gain,
    norm1_bias,
    query_bias,
    value_bias,
    proj_bias,
    norm2_gain,
    norm2_bias,
    up_bias,
    down_bias,
):
    gathered = (
        lax.all_gather(qkv_weight, ("rows", "cols"), axis=0, tiled=True),
        lax.all_gather(proj_weight, ("rows", "cols"), axis=0, tiled=True),
        lax.all_gather(up_weight, ("rows", "cols"), axis=0, tiled=True),
        lax.all_gather(down_weight, ("rows", "cols"), axis=0, tiled=True),
        lax.all_gather(norm1_gain, ("rows", "cols"), axis=0, tiled=True),
        lax.all_gather(norm1_bias, ("rows", "cols"), axis=0, tiled=True),
        lax.all_gather(query_bias, ("rows", "cols"), axis=0, tiled=True),
        lax.all_gather(value_bias, ("rows", "cols"), axis=0, tiled=True),
        lax.all_gather(proj_bias, ("rows", "cols"), axis=0, tiled=True),
        lax.all_gather(norm2_gain, ("rows", "cols"), axis=0, tiled=True),
        lax.all_gather(norm2_bias, ("rows", "cols"), axis=0, tiled=True),
        lax.all_gather(up_bias, ("rows", "cols"), axis=0, tiled=True),
        lax.all_gather(down_bias, ("rows", "cols"), axis=0, tiled=True),
    )
    (
        qkv_full,
        proj_full,
        up_full,
        down_full,
        gain_one_full,
        bias_one_full,
        query_add,
        value_add,
        proj_add,
        gain_two_full,
        bias_two_full,
        up_add,
        down_add,
    ) = gathered
    tokens_tile, grad_tile = roll_in(images, cotangent)
    image_count, tile_side, features = (
        tokens_tile.shape[0],
        tokens_tile.shape[1],
        tokens_tile.shape[3],
    )
    window = tile_side * tile_side
    row_total = image_count * window
    tokens = tokens_tile.reshape(row_total, features)
    grad_rows = grad_tile.reshape(row_total, features)
    local_pos = jnp.arange(tile_side, dtype=jnp.int32)
    band_rows = band_of(
        lax.axis_index("rows") * tile_side + local_pos, lax.axis_size("rows") * tile_side
    )
    band_cols = band_of(
        lax.axis_index("cols") * tile_side + local_pos, lax.axis_size("cols") * tile_side
    )
    region = (3 * band_rows[:, None] + band_cols[None, :]).reshape(window)
    allowed = (region[:, None] == region[None, :])[None, None]
    head_count = rel_table.shape[1]
    table_size = rel_table.shape[0]
    head_width = features // head_count
    score_scale = head_width ** (-0.5)
    onehot = (
        rel_index.reshape(window * window)[:, None]
        == jnp.arange(table_size, dtype=jnp.int32)[None, :]
    ).astype(jnp.float32)
    bias_flat = jnp.dot(
        onehot, rel_table, precision=lax.Precision.HIGHEST, preferred_element_type=jnp.float32
    )
    bias_heads = bias_flat.T.reshape(head_count, window, window)

    def split_heads(values):
        return values.reshape(image_count, window, head_count, head_width)

    def scores_of(query_b, key_b):
        raw_scores = jnp.einsum(
            "wqhd,wkhd->whqk",
            split_heads(query_b),
            split_heads(key_b),
            preferred_element_type=jnp.float32,
        )
        return jnp.where(allowed, raw_scores + bias_heads[None], big_negative)

    gain_one = gain_one_full.astype(jnp.float32)
    gain_two = gain_two_full.astype(jnp.float32)
    out_one, normed_one, inv_one = layer_norm(tokens, gain_one, bias_one_full.astype(jnp.float32))
    h_one = out_one.astype(jnp.bfloat16)
    projected = dot_plain(h_one, qkv_full)
    query_b = ((projected[:, :features] + query_add.astype(jnp.float32)) * score_scale).astype(
        jnp.bfloat16
    )
    key_b = projected[:, features : 2 * features].astype(jnp.bfloat16)
    value_b = (projected[:, 2 * features :] + value_add.astype(jnp.float32)).astype(jnp.bfloat16)
    scores = scores_of(query_b, key_b)
    row_top = jnp.max(scores, axis=-1, keepdims=True)
    log_total = row_top + jnp.log(jnp.sum(jnp.exp(scores - row_top), axis=-1, keepdims=True))
    attend_b = jnp.exp(scores - log_total).astype(jnp.bfloat16)
    attn_b = (
        jnp.einsum(
            "whqk,wkhd->wqhd", attend_b, split_heads(value_b), preferred_element_type=jnp.float32
        )
        .reshape(row_total, features)
        .astype(jnp.bfloat16)
    )
    residual = tokens + dot_plain(attn_b, proj_full) + proj_add.astype(jnp.float32)
    out_two, normed_two, inv_two = layer_norm(residual, gain_two, bias_two_full.astype(jnp.float32))
    h_two = out_two.astype(jnp.bfloat16)
    hidden_pre = dot_plain(h_two, up_full) + up_add.astype(jnp.float32)
    gauss_cdf = 0.5 * (1.0 + lax.erf(hidden_pre * root_half))
    act_b = (hidden_pre * gauss_cdf).astype(jnp.bfloat16)
    result = residual + dot_plain(act_b, down_full) + down_add.astype(jnp.float32)
    regathered = (
        lax.all_gather(qkv_weight, ("rows", "cols"), axis=0, tiled=True),
        lax.all_gather(proj_weight, ("rows", "cols"), axis=0, tiled=True),
        lax.all_gather(up_weight, ("rows", "cols"), axis=0, tiled=True),
        lax.all_gather(down_weight, ("rows", "cols"), axis=0, tiled=True),
        lax.all_gather(norm1_gain, ("rows", "cols"), axis=0, tiled=True),
        lax.all_gather(norm1_bias, ("rows", "cols"), axis=0, tiled=True),
        lax.all_gather(query_bias, ("rows", "cols"), axis=0, tiled=True),
        lax.all_gather(value_bias, ("rows", "cols"), axis=0, tiled=True),
        lax.all_gather(proj_bias, ("rows", "cols"), axis=0, tiled=True),
        lax.all_gather(norm2_gain, ("rows", "cols"), axis=0, tiled=True),
        lax.all_gather(norm2_bias, ("rows", "cols"), axis=0, tiled=True),
        lax.all_gather(up_bias, ("rows", "cols"), axis=0, tiled=True),
        lax.all_gather(down_bias, ("rows", "cols"), axis=0, tiled=True),
    )
    qkv_back, proj_back, up_back, down_back = (
        regathered[0],
        regathered[1],
        regathered[2],
        regathered[3],
    )
    gain_one_back = regathered[4].astype(jnp.float32)
    gain_two_back = regathered[9].astype(jnp.float32)
    grad_b = grad_rows.astype(jnp.bfloat16)
    grad_down = dot_lead(act_b, grad_b)
    grad_down_add = jnp.sum(grad_rows, axis=0)
    grad_act = dot_tail(grad_b, down_back)
    density = jnp.exp(-0.5 * hidden_pre * hidden_pre) * tau_factor
    grad_pre = grad_act * (gauss_cdf + hidden_pre * density)
    grad_pre_b = grad_pre.astype(jnp.bfloat16)
    grad_up = dot_lead(h_two, grad_pre_b)
    grad_up_add = jnp.sum(grad_pre, axis=0)
    grad_h_two = dot_tail(grad_pre_b, up_back)
    grad_resid, grad_gain_two, grad_bias_two = norm_back(
        grad_h_two, normed_two, inv_two, gain_two_back
    )
    grad_resid = grad_resid + grad_rows
    grad_resid_b = grad_resid.astype(jnp.bfloat16)
    grad_proj = dot_lead(attn_b, grad_resid_b)
    grad_proj_add = jnp.sum(grad_resid, axis=0)
    grad_attn_b = dot_tail(grad_resid_b, proj_back).astype(jnp.bfloat16)
    grad_heads = split_heads(grad_attn_b)
    grad_attend = jnp.einsum(
        "wqhd,wkhd->whqk", grad_heads, split_heads(value_b), preferred_element_type=jnp.float32
    )
    attend = jnp.exp(scores_of(query_b, key_b) - log_total)
    grad_value = jnp.einsum(
        "whqk,wqhd->wkhd",
        attend.astype(jnp.bfloat16),
        grad_heads,
        preferred_element_type=jnp.float32,
    ).reshape(row_total, features)
    row_inner = jnp.sum(attend * grad_attend, axis=-1, keepdims=True)
    grad_scores = attend * (grad_attend - row_inner)
    grad_bias_heads = jnp.sum(grad_scores, axis=0).reshape(head_count, window * window)
    table_local = lax.dot_general(
        onehot,
        grad_bias_heads,
        (((0,), (1,)), ((), ())),
        precision=lax.Precision.HIGHEST,
        preferred_element_type=jnp.float32,
    )
    grad_scores_b = grad_scores.astype(jnp.bfloat16)
    grad_query = (
        jnp.einsum(
            "whqk,wkhd->wqhd", grad_scores_b, split_heads(key_b), preferred_element_type=jnp.float32
        )
        * score_scale
    ).reshape(row_total, features)
    grad_key = jnp.einsum(
        "whqk,wqhd->wkhd", grad_scores_b, split_heads(query_b), preferred_element_type=jnp.float32
    ).reshape(row_total, features)
    grad_query_add = jnp.sum(grad_query, axis=0)
    grad_value_add = jnp.sum(grad_value, axis=0)
    grad_mixed_b = jnp.concatenate([grad_query, grad_key, grad_value], axis=1).astype(jnp.bfloat16)
    grad_qkv = dot_lead(h_one, grad_mixed_b)
    grad_h_one = dot_tail(grad_mixed_b, qkv_back)
    grad_in, grad_gain_one, grad_bias_one = norm_back(
        grad_h_one, normed_one, inv_one, gain_one_back
    )
    grad_tokens = grad_resid + grad_in
    grad_table = lax.psum(table_local, ("rows", "cols"))
    shard_grads = (
        lax.psum_scatter(grad_qkv, ("rows", "cols"), scatter_dimension=0, tiled=True),
        lax.psum_scatter(grad_proj, ("rows", "cols"), scatter_dimension=0, tiled=True),
        lax.psum_scatter(grad_up, ("rows", "cols"), scatter_dimension=0, tiled=True),
        lax.psum_scatter(grad_down, ("rows", "cols"), scatter_dimension=0, tiled=True),
        lax.psum_scatter(grad_gain_one, ("rows", "cols"), scatter_dimension=0, tiled=True),
        lax.psum_scatter(grad_bias_one, ("rows", "cols"), scatter_dimension=0, tiled=True),
        lax.psum_scatter(grad_query_add, ("rows", "cols"), scatter_dimension=0, tiled=True),
        lax.psum_scatter(grad_value_add, ("rows", "cols"), scatter_dimension=0, tiled=True),
        lax.psum_scatter(grad_proj_add, ("rows", "cols"), scatter_dimension=0, tiled=True),
        lax.psum_scatter(grad_gain_two, ("rows", "cols"), scatter_dimension=0, tiled=True),
        lax.psum_scatter(grad_bias_two, ("rows", "cols"), scatter_dimension=0, tiled=True),
        lax.psum_scatter(grad_up_add, ("rows", "cols"), scatter_dimension=0, tiled=True),
        lax.psum_scatter(grad_down_add, ("rows", "cols"), scatter_dimension=0, tiled=True),
    )
    block_out, grad_images = roll_out(
        result.reshape(image_count, tile_side, tile_side, features),
        grad_tokens.reshape(image_count, tile_side, tile_side, features),
    )
    return (
        block_out,
        grad_images,
        shard_grads[0],
        shard_grads[1],
        shard_grads[2],
        shard_grads[3],
        shard_grads[4],
        shard_grads[5],
        shard_grads[6],
        shard_grads[7],
        shard_grads[8],
        shard_grads[9],
        shard_grads[10],
        shard_grads[11],
        shard_grads[12],
        grad_table,
    )


def solution(mesh):
    in_specs = (
        P(None, "rows", "cols", None),
        P(None, "rows", "cols", None),
        P(),
        P(),
        P(("rows", "cols"), None),
        P(("rows", "cols"), None),
        P(("rows", "cols"), None),
        P(("rows", "cols"), None),
        P(("rows", "cols")),
        P(("rows", "cols")),
        P(("rows", "cols")),
        P(("rows", "cols")),
        P(("rows", "cols")),
        P(("rows", "cols")),
        P(("rows", "cols")),
        P(("rows", "cols")),
        P(("rows", "cols")),
    )
    out_specs = (
        P(None, "rows", "cols", None),
        P(None, "rows", "cols", None),
        P(("rows", "cols"), None),
        P(("rows", "cols"), None),
        P(("rows", "cols"), None),
        P(("rows", "cols"), None),
        P(("rows", "cols")),
        P(("rows", "cols")),
        P(("rows", "cols")),
        P(("rows", "cols")),
        P(("rows", "cols")),
        P(("rows", "cols")),
        P(("rows", "cols")),
        P(("rows", "cols")),
        P(("rows", "cols")),
        P(),
    )
    return jax.shard_map(
        per_device, mesh=mesh, in_specs=in_specs, out_specs=out_specs, check_vma=False
    )
```

profile of v0, /device:TPU:0, one launch (start us, length us, event | category | flops | bytes accessed | tf_op | source)
XLA Modules:
  0.0 750.2 jit_solution(12230946306271899219)
XLA Ops:
  9.8 3.4 collective-permute-start.4
  16.0 72.4 %all_gather.50 = bf16[512,512]{1,0:T(8,128)(2,1)S(1)} all-gather(bf16[16,512]{1,0:T(8,128)(2,1)} %param.22), channel_id=1, replica_groups=mesh['rows'=8,'cols'=4] {'rows','cols'}, dimensions={0}, use_global_device_ids=true | all-gather | bytes 540672 | tf_op jit(solution)/shard_map/all_gather | solution.py:118
  88.4 1.3 convolution_bitcast_fusion
  92.1 37.4 %all-reduce.19 = (bf16[512]{0:T(512)(128)(2,1)S(1)}, bf16[512]{0:T(512)(128)(2,1)S(1)}, bf16[512]{0:T(512)(128)(2,1)S(1)}, bf16[512]{0:T(512)(128)(2,1)S(1)}, bf...) all-reduce(bf16[512]{0:T(512)(128)(2,1)S(1)} %dynamic-update-slice., ...), channel_id=1, replica_groups=mesh['rows'=8,'cols'=4] {'rows','cols'}, use_global_device_ids=true, to_apply=%add.1 | all-reduce | flops 6144 | bytes 24576
  131.4 2.2 collective-permute-start.1
  133.6 2.2 collective-permute-start.5
  136.5 2.8 collective-permute-done.1
  140.3 1.7 collective-permute-done.5
  143.3 1.9 fusion.42
  145.9 1.5 copy.84
  147.9 1.5 copy.85
  149.9 1.6 copy.87
  151.4 2.0 fusion.50
  154.9 1.2 copy.89
  156.1 1.4 convert_element_type.133
  158.3 3.6 multiply_convert_fusion
  161.8 24.8 %all-gather.8.cloned.1.call-done = bf16[2048,512]{1,0:T(8,128)(2,1)} async-done(((bf16[64,512]{1,0:T(8,128)(2,1)}), bf16[2048,512]{1,0:T(8,128)(2,1)}) %all-gather.8.cloned.1.call-update) | async-done | bytes 2097168 | tf_op jit(solution)/shard_map/all_gather | solution.py:120
  186.7 4.0 fusion.52
  190.7 1.5 multiply_reduce_fusion.1
  193.0 1.0 convolution_convert_fusion.2
  194.0 1.3 fusion.32
  195.3 2.3 reshape.268
  197.6 2.6 copy.92
  200.5 2.3 fusion.48
  202.8 1.2 copy.102
  204.0 2.1 reshape.244
  206.1 1.9 multiply_reduce_fusion
  208.0 1.4 fusion.44
  211.0 1.2 copy.99
  212.2 2.1 reshape.243
  214.3 1.1 fusion.49
  218.8 2.5 fusion.41
  221.4 1.1 copy-done.18
  222.4 2.8 fusion.20
  226.3 2.7 fusion.35
  230.6 3.0 fusion.11
  233.6 1.1 reshape.239
  235.4 2.3 multiply_reduce_fusion.2
  239.2 39.7 %all-reduce.18 = (f32[512]{0:T(512)S(1)}, f32[512]{0:T(512)S(1)}, f32[512]{0:T(512)S(1)}, f32[512]{0:T(512)S(1)}, f32[512]{0:T(512)S(1)}, /*index=5*/f32[512]{0:...) all-reduce(f32[512]{0:T(512)S(1)} %get-tuple-element.50, ...), channel_id=6, replica_groups=mesh['rows'=8,'cols'=4] {'rows','cols'}, use_global_device_ids=true, to_apply=%region_16.17.clone | all-reduce | flops 8848 | bytes 70784
  284.7 1.6 collective-permute-start.3
  286.2 2.3 collective-permute-done.6
  288.7 1.6 collective-permute-start.7
  290.3 2.4 collective-permute-done.3
  293.8 2.3 collective-permute-done.7
  297.2 39.5 %reduce-scatter.7.cloned.1.call-done = f32[16,512]{1,0:T(8,128)} async-done(((f32[512,512]{1,0:T(8,128)}), f32[16,512]{1,0:T(8,128)}) %reduce-scatter.7.cloned.1.call-update) | async-done | bytes 32784 | tf_op jit(solution)/shard_map/reduce_scatter | solution.py:302
  336.8 104.7 %reduce-scatter.5.cloned.1.call-done = f32[16,1536]{1,0:T(8,128)} async-done(((f32[512,1536]{1,0:T(8,128)}), f32[16,1536]{1,0:T(8,128)}) %reduce-scatter.5.cloned.1.call-update) | async-done | bytes 98320 | tf_op jit(solution)/shard_map/reduce_scatter | solution.py:301
  441.5 151.3 %reduce-scatter.9.cloned.1.call-done = f32[16,2048]{1,0:T(8,128)} async-done(((f32[512,2048]{1,0:T(8,128)}), f32[16,2048]{1,0:T(8,128)}) %reduce-scatter.9.cloned.1.call-update) | async-done | bytes 131088 | tf_op jit(solution)/shard_map/reduce_scatter | solution.py:303
  592.8 150.6 %reduce-scatter.11.cloned.1.call-done = f32[64,512]{1,0:T(8,128)} async-done(((f32[2048,512]{1,0:T(8,128)}), f32[64,512]{1,0:T(8,128)}) %reduce-scatter.11.cloned.1.call-update) | async-done | bytes 131088 | tf_op jit(solution)/shard_map/reduce_scatter | solution.py:304
  (235 shorter events, 34.8 us)
Async XLA Ops:
  7.2 81.2 %copy-start = (f32[169,16]{0,1:T(8,128)S(1)}, f32[169,16]{0,1:T(8,128)}, u32[]{:S(2)}) copy-start(f32[169,16]{0,1:T(8,128)} %param.20) | copy-start | bytes 32452
  7.2 82.5 %copy-start.22 = (f32[4,7,7,512]{3,0,2,1:T(4,128)S(1)}, f32[4,7,7,512]{3,0,2,1:T(4,128)}, u32[]{:S(2)}) copy-start(f32[4,7,7,512]{3,0,2,1:T(4,128)} %param.18) | copy-start | bytes 1204228
  7.2 82.5 %copy-start.21 = (f32[4,7,7,512]{3,0,2,1:T(4,128)S(1)}, f32[4,7,7,512]{3,0,2,1:T(4,128)}, u32[]{:S(2)}) copy-start(f32[4,7,7,512]{3,0,2,1:T(4,128)} %param.17) | copy-start | bytes 1204228
  7.2 82.6 %copy-start.43 = (bf16[16]{0:T(256)(128)(2,1)S(1)}, bf16[16]{0:T(256)(128)(2,1)}, u32[]{:S(2)}) copy-start(bf16[16]{0:T(256)(128)(2,1)} %param.30) | copy-start | bytes 100
  7.2 82.8 %copy-start.44 = (bf16[16]{0:T(256)(128)(2,1)S(1)}, bf16[16]{0:T(256)(128)(2,1)}, u32[]{:S(2)}) copy-start(bf16[16]{0:T(256)(128)(2,1)} %param.31) | copy-start | bytes 100
  7.2 83.1 %copy-start.45 = (bf16[16]{0:T(256)(128)(2,1)S(1)}, bf16[16]{0:T(256)(128)(2,1)}, u32[]{:S(2)}) copy-start(bf16[16]{0:T(256)(128)(2,1)} %param.29) | copy-start | bytes 100
  7.2 83.3 %copy-start.46 = (bf16[16]{0:T(256)(128)(2,1)S(1)}, bf16[16]{0:T(256)(128)(2,1)}, u32[]{:S(2)}) copy-start(bf16[16]{0:T(256)(128)(2,1)} %param.27) | copy-start | bytes 100
  7.3 83.5 %copy-start.47 = (bf16[16]{0:T(256)(128)(2,1)S(1)}, bf16[16]{0:T(256)(128)(2,1)}, u32[]{:S(2)}) copy-start(bf16[16]{0:T(256)(128)(2,1)} %param.28) | copy-start | bytes 100
  7.3 83.8 %copy-start.48 = (bf16[16]{0:T(256)(128)(2,1)S(1)}, bf16[16]{0:T(256)(128)(2,1)}, u32[]{:S(2)}) copy-start(bf16[16]{0:T(256)(128)(2,1)} %param.25) | copy-start | bytes 100
  7.3 84.0 %copy-start.49 = (bf16[16]{0:T(256)(128)(2,1)S(1)}, bf16[16]{0:T(256)(128)(2,1)}, u32[]{:S(2)}) copy-start(bf16[16]{0:T(256)(128)(2,1)} %param.26) | copy-start | bytes 100
  7.3 84.3 %copy-start.50 = (bf16[16]{0:T(256)(128)(2,1)S(1)}, bf16[16]{0:T(256)(128)(2,1)}, u32[]{:S(2)}) copy-start(bf16[16]{0:T(256)(128)(2,1)} %param.33) | copy-start | bytes 100
  7.3 84.5 %copy-start.51 = (bf16[64]{0:T(256)(128)(2,1)S(1)}, bf16[64]{0:T(256)(128)(2,1)}, u32[]{:S(2)}) copy-start(bf16[64]{0:T(256)(128)(2,1)} %param.32) | copy-start | bytes 388
  7.3 136.0 %all-gather.4.cloned.1.call-start = ((), (), s32[]{:S(2)}) async-start(), calls=%async_computation.4 | async-start | bytes 1622016 | tf_op jit(solution)/shard_map/all_gather | solution.py:117
  8.0 150.2 %all-gather.6.cloned.1.call-start = ((), (), s32[]{:S(2)}) async-start(), calls=%async_computation.5 | async-start | bytes 2162688 | tf_op jit(solution)/shard_map/all_gather | solution.py:119
  8.8 177.9 %all-gather.8.cloned.1.call-start = ((), (), s32[]{:S(2)}) async-start(), calls=%async_computation.6 | async-start | bytes 2162688 | tf_op jit(solution)/shard_map/all_gather | solution.py:120
  9.8 123.8 %collective-permute-start.4 = (f32[4,3,7,512]{3,0,2,1:T(4,128)S(1)}, f32[4,3,7,512]{3,0,2,1:T(4,128)S(1)}, u32[]{:S(2)}, u32[]{:S(2)}) collective-permute-start(f32[4,3,7,512]{3,0,2,1:T(4,128)S(1)} %slice.74), channel_id=1, source_target_pairs={{0,28},{4,0},{8,4},{12,8},{16,12},{20,16},{24,20},{28,24},{1,29},{... | collective-permute-start | bytes 516104 | tf_op jit(solution)/shard_map/ppermute | solution.py:18
  14.1 117.2 %collective-permute-start = (f32[4,3,7,512]{3,0,2,1:T(4,128)S(1)}, f32[4,3,7,512]{3,0,2,1:T(4,128)S(1)}, u32[]{:S(2)}, u32[]{:S(2)}) collective-permute-start(f32[4,3,7,512]{3,0,2,1:T(4,128)S(1)} %slice.63), channel_id=1, source_target_pairs={{0,28},{4,0},{8,4},{12,8},{16,12},{20,16},{24,20},{28,24},{1,29},{... | collective-permute-start | bytes 516104 | tf_op jit(solution)/shard_map/ppermute | solution.py:18
  14.9 321.9 %reduce-scatter.7.cloned.1.call-start = ((), (), s32[]{:S(2)}) async-start(), calls=%async_computation.8 | async-start | bytes 1081344 | tf_op jit(solution)/shard_map/reduce_scatter | solution.py:302
  16.0 75.6 %copy-start.33 = (s32[2401]{0:T(1024)}, s32[2401]{0:T(1024)S(1)}, u32[]{:S(2)}) copy-start(s32[2401]{0:T(1024)S(1)} %eq.35) | copy-start | bytes 28816
  88.4 69.2 %copy-start.5 = (bf16[512,512]{1,0:T(8,128)(2,1)}, bf16[512,512]{1,0:T(8,128)(2,1)S(1)}, u32[]{:S(2)}) copy-start(bf16[512,512]{1,0:T(8,128)(2,1)S(1)} %all_gather.50) | copy-start | bytes 1572868
  129.5 89.3 %copy-start.25 = (f32[512]{0:T(512)}, f32[512]{0:T(512)S(1)}, u32[]{:S(2)}) copy-start(f32[512]{0:T(512)S(1)} %convert_element_type.119) | copy-start | bytes 6148
  131.4 7.9 %collective-permute-start.1 = (f32[4,7,3,512]{3,0,2,1:T(4,128)S(1)}, f32[4,7,3,512]{3,0,2,1:T(4,128)S(1)}, u32[]{:S(2)}, u32[]{:S(2)}) collective-permute-start(f32[4,7,3,512]{3,0,2,1:T(4,128)S(1)} %pad_maximum_fusion.5), channel_id=1, source_target_pairs={{0,3},{1,0},{2,1},{3,2},{4,7},{5,4},{6,5},{7,6},{8,11},{9,8},{10,9... | collective-permute-start | bytes 516104 | tf_op jit(solution)/shard_map/ppermute | solution.py:18
  133.6 8.4 %collective-permute-start.5 = (f32[4,7,3,512]{3,0,2,1:T(4,128)S(1)}, f32[4,7,3,512]{3,0,2,1:T(4,128)S(1)}, u32[]{:S(2)}, u32[]{:S(2)}) collective-permute-start(f32[4,7,3,512]{3,0,2,1:T(4,128)S(1)} %pad_maximum_fusion.4), channel_id=1, source_target_pairs={{0,3},{1,0},{2,1},{3,2},{4,7},{5,4},{6,5},{7,6},{8,11},{9,8},{10,9... | collective-permute-start | bytes 516104 | tf_op jit(solution)/shard_map/ppermute | solution.py:18
  139.7 3.6 copy-start.27
  140.3 3.1 copy-start.30
  154.5 3.0 copy-start.37
  186.7 4.0 copy-start.14
  190.7 2.3 copy-start.6
  192.2 1.8 copy-start.13
  200.2 241.3 %reduce-scatter.5.cloned.1.call-start = ((), (), s32[]{:S(2)}) async-start(), calls=%async_computation.7 | async-start | bytes 3244032 | tf_op jit(solution)/shard_map/reduce_scatter | solution.py:301
  208.0 2.4 copy-start.9
  210.4 3.9 copy-start.8
  211.0 3.3 copy-start.2
  215.4 3.4 copy-start.16
  215.4 3.4 copy-start.28
  215.4 3.4 copy-start.31
  221.3 371.5 %reduce-scatter.9.cloned.1.call-start = ((), (), s32[]{:S(2)}) async-start(), calls=%async_computation.9 | async-start | bytes 4325376 | tf_op jit(solution)/shard_map/reduce_scatter | solution.py:303
  225.3 518.1 %reduce-scatter.11.cloned.1.call-start = ((), (), s32[]{:S(2)}) async-start(), calls=%async_computation.10 | async-start | bytes 4325376 | tf_op jit(solution)/shard_map/reduce_scatter | solution.py:304
  230.6 4.4 copy-start.15
  234.6 49.9 %collective-permute-start.2 = (bf16[4,3,7,512]{3,2,1,0:T(8,128)(2,1)S(1)}, bf16[4,3,7,512]{3,2,1,0:T(8,128)(2,1)S(1)}, u32[]{:S(2)}, u32[]{:S(2)}) collective-permute-start(bf16[4,3,7,512]{3,2,1,0:T(8,128)(2,1)S(1)} %slice.137), channel_id=1, source_target_pairs={{0,4},{4,8},{8,12},{12,16},{16,20},{20,24},{24,28},{28,0},{1,5},{5... | collective-permute-start | bytes 258056 | tf_op jit(solution)/shard_map/ppermute | solution.py:18
  235.2 2.5 copy-start.4
  235.2 2.5 copy-start.26
  235.2 2.5 copy-start.29
  235.2 2.5 copy-start.32
  235.4 2.6 copy-start.34
  283.6 5.0 collective-permute-start.6
  284.7 8.0 %collective-permute-start.3 = (bf16[4,7,3,512]{3,2,1,0:T(4,128)(2,1)S(1)}, bf16[4,7,3,512]{3,2,1,0:T(4,128)(2,1)S(1)}, u32[]{:S(2)}, u32[]{:S(2)}) collective-permute-start(bf16[4,7,3,512]{3,2,1,0:T(4,128)(2,1)S(1)} %fusion.29), channel_id=1, source_target_pairs={{0,1},{1,2},{2,3},{3,0},{4,5},{5,6},{6,7},{7,4},{8,9},{9,10},{10,1... | collective-permute-start | bytes 258056 | tf_op jit(solution)/shard_map/ppermute | solution.py:18
  288.7 7.4 collective-permute-start.7
  (19 other events, 21.5 us)
Sparse Core Ops, SparseCore 0:
  11.0 57.9 all-gather.3
  72.0 55.4 all-gather.5
  130.4 56.1 all-gather.7
  200.3 136.3 reduce-scatter.6
  342.6 98.8 reduce-scatter.4
  444.2 148.5 reduce-scatter.8
  595.6 147.6 reduce-scatter.10
where the time goes:
time: 751 us; the launch traced here: 750 us
  waiting for transfers between devices  484 us (64%)
  blocking collectives  150 us (20%)
  local copies, waits for them, and re-layouts  45.1 us (6%)
  matrix products  37.5 us (5%)
  between operations  15 us (2%)
  starting transfers between devices  12.8 us (2%)
    reduce_scatter x1, waiting for transfers between devices, per_device(): lax.psum_scatter(grad_up, ('rows', 'cols'), scatter_dimension=0, tiled=True)  151 us
    reduce_scatter x1, waiting for transfers between devices, per_device(): lax.psum_scatter(grad_down, ('rows', 'cols'), scatter_dimension=0, tiled=...  151 us
    reduce_scatter x1, waiting for transfers between devices, per_device(): lax.psum_scatter(grad_qkv, ('rows', 'cols'), scatter_dimension=0, tiled=T...  105 us
    unnamed x2, blocking collectives  77.1 us
    all_gather x1, blocking collectives, per_device(): lax.all_gather(proj_weight, ('rows', 'cols'), axis=0, tiled=True)  72.4 us
    reduce_scatter x1, waiting for transfers between devices, per_device(): lax.psum_scatter(grad_proj, ('rows', 'cols'), scatter_dimension=0, tiled=...  39.5 us
    all_gather x1, waiting for transfers between devices, per_device(): lax.all_gather(down_weight, ('rows', 'cols'), axis=0, tiled=True)  24.8 us
    unnamed x135, local copies, waits for them, and re-layouts  16.1 us
  transfers between devices with their start and end apart: 15, of which 10 were waited for; matrix products, arithmetic and copies ran while one was open for 9% of the time, Pallas kernels for 0%

commit v1 on v0

--- a/solution.py
+++ b/solution.py
@@ -1,6 +1,10 @@
+import functools
+
 import jax
 import jax.numpy as jnp
 from jax import lax
+from jax.experimental import pallas as pl
+from jax.experimental.pallas import tpu as pltpu
 from jax.sharding import PartitionSpec as P
 
 WIN = 7
@@ -92,6 +96,363 @@
         jnp.concatenate([beside[0], tall_result[:, :, :-SHIFT]], axis=2),
         jnp.concatenate([beside[1], tall_grads[:, :, :-SHIFT]], axis=2),
     )
+
+
+MESH = pl.DeviceIdType.MESH
+CORES = 2
+
+
+def grid_of(rows):
+    chips = rows // CORES
+    across = 1
+    for size in range(1, chips + 1):
+        if chips % size == 0 and size * size <= chips:
+            across = size
+    return chips // across, across
+
+
+def whereabouts(dims):
+    height, width = dims[0], dims[1]
+    row, depth_at = lax.axis_index("rows"), lax.axis_index("cols")
+    core = lax.rem(row, CORES)
+    chip = row // CORES
+    return chip // width, lax.rem(chip, width), core, depth_at
+
+
+def device_at(dims, y, x, core, z):
+    return ((y * dims[1] + x) * CORES + core, z)
+
+
+def greet(dims, here):
+    barrier = pltpu.get_barrier_semaphore()
+    total = 0
+    for axis in range(4):
+        for step in range(1, dims[axis]):
+            there = list(here)
+            there[axis] = lax.rem(here[axis] + step, dims[axis])
+            pl.semaphore_signal(
+                barrier, inc=1, device_id=device_at(dims, *there), device_id_type=MESH
+            )
+            total += 1
+    pl.semaphore_wait(barrier, total)
+
+
+def moved(here, axis, step, dims):
+    there = list(here)
+    there[axis] = lax.rem(here[axis] + step, dims[axis])
+    return there
+
+
+def gather_kernel(dims, count, *refs):
+    ins, outs = refs[:count], refs[count : 2 * count]
+    local_sem, send_sem, recv_sem = refs[2 * count :]
+    height, width, _, depth = dims
+    here = whereabouts(dims)
+    y, x, core, z = here
+    greet(dims, here)
+    used = [0] * count
+
+    def send(stream, src, dst, there):
+        slot = used[stream]
+        used[stream] += 1
+        copy = pltpu.make_async_remote_copy(
+            src_ref=src,
+            dst_ref=dst,
+            send_sem=send_sem.at[stream, slot],
+            recv_sem=recv_sem.at[stream, slot],
+            device_id=device_at(dims, *there),
+            device_id_type=MESH,
+        )
+        copy.start()
+        return copy
+
+    started = []
+    along_z, locals_ = [], []
+    for k in range(count):
+        mine = pltpu.make_async_copy(ins[k], outs[k].at[y, x, core, z], local_sem.at[k])
+        mine.start()
+        locals_.append(mine)
+        along_z.append(
+            [
+                send(k, ins[k], outs[k].at[y, x, core, z], moved(here, 3, step, dims))
+                for step in range(1, depth)
+            ]
+        )
+        started += along_z[k]
+    first, second, partner = [], [], []
+    other = moved(here, 2, 1, dims)
+    for k in range(count):
+        locals_[k].wait()
+        for copy in along_z[k]:
+            copy.wait_recv()
+        axis = k % 2
+        block = outs[k].at[y, x, core]
+        first.append(
+            [send(k, block, block, moved(here, axis, s, dims)) for s in range(1, dims[axis])]
+        )
+        partner.append([send(k, block, block, other)])
+        started += first[k] + partner[k]
+    for k in range(count):
+        axis = k % 2
+        cross = 1 - axis
+        for copy in first[k]:
+            copy.wait_recv()
+        copies = []
+        for lag in range(dims[axis]):
+            at = moved(here, axis, lag, dims)
+            block = outs[k].at[at[0], at[1], core]
+            copies += [
+                send(k, block, block, moved(here, cross, s, dims)) for s in range(1, dims[cross])
+            ]
+            if lag:
+                partner[k].append(send(k, block, block, other))
+                started.append(partner[k][-1])
+        second.append(copies)
+        started += copies
+    for k in range(count):
+        axis = k % 2
+        cross = 1 - axis
+        copies = iter(second[k])
+        for lag in range(dims[axis]):
+            for s in range(1, dims[cross]):
+                next(copies).wait_recv()
+                at = moved(here, axis, lag, dims)
+                at[cross] = lax.rem(here[cross] + dims[cross] - s, dims[cross])
+                block = outs[k].at[at[0], at[1], core]
+                partner[k].append(send(k, block, block, other))
+                started.append(partner[k][-1])
+    for k in range(count):
+        for copy in partner[k]:
+            copy.wait_recv()
+    for copy in started:
+        copy.wait_send()
+
+
+def reduce_kernel(dims, count, *refs):
+    ins, table = refs[:count], refs[count]
+    outs, table_out = refs[count + 1 : 2 * count + 1], refs[2 * count + 1]
+    rest = refs[2 * count + 2 :]
+    bufs = [rest[7 * k : 7 * k + 7] for k in range(count)]
+    table_in = rest[7 * count : 7 * count + 4]
+    table_sum = rest[7 * count + 4 : 7 * count + 7]
+    send_sem, recv_sem = rest[7 * count + 7 :]
+    height, width, _, depth = dims
+    here = whereabouts(dims)
+    y, x, core, z = here
+    greet(dims, here)
+    used = [0] * (count + 1)
+    started = []
+
+    def send(stream, src, dst, there):
+        slot = used[stream]
+        used[stream] += 1
+        copy = pltpu.make_async_remote_copy(
+            src_ref=src,
+            dst_ref=dst,
+            send_sem=send_sem.at[stream, slot],
+            recv_sem=recv_sem.at[stream, slot],
+            device_id=device_at(dims, *there),
+            device_id_type=MESH,
+        )
+        copy.start()
+        started.append(copy)
+        return copy
+
+    def add(dst, parts):
+        def body(i, carry):
+            total = parts[0][i].astype(jnp.float32)
+            for part in parts[1:]:
+                total = total + part[i].astype(jnp.float32)
+            dst[i] = total.astype(dst.dtype)
+            return carry
+
+        lax.fori_loop(0, depth, body, 0)
+
+    def table_step(stage, axis, src):
+        table_in[stage][here[axis]] = src[...]
+        return [
+            send(count, src, table_in[stage].at[here[axis]], moved(here, axis, s, dims))
+            for s in range(1, dims[axis])
+        ]
+
+    def table_add(stage, axis, copies, dst):
+        for copy in copies:
+            copy.wait_recv()
+        total = table_in[stage][0]
+        for j in range(1, dims[axis]):
+            total = total + table_in[stage][j]
+        dst[...] = total
+
+    other = moved(here, 2, 1, dims)
+    table_copies = table_step(0, 2, table)
+    core_copies = []
+    for k in range(count):
+        axis = k % 2
+        cross = 1 - axis
+        group = {}
+        for lag in list(range(1, dims[axis])) + [0]:
+            for j in range(dims[cross]):
+                at = moved(here, axis, lag, dims)
+                at[cross] = j
+                group[lag, j] = send(
+                    k, ins[k].at[at[0], at[1], other[2]], bufs[k][0].at[at[0], at[1]], other
+                )
+        core_copies.append(group)
+    table_add(0, 2, table_copies, table_sum[0])
+    table_copies = table_step(1, 0, table_sum[0])
+    first = []
+    for k in range(count):
+        axis = k % 2
+        cross = 1 - axis
+        from_core, sum_core, from_first = bufs[k][0], bufs[k][1], bufs[k][2]
+        group = []
+        for lag in list(range(1, dims[axis])) + [0]:
+            for j in range(dims[cross]):
+                at = moved(here, axis, lag, dims)
+                at[cross] = j
+                core_copies[k][lag, j].wait_recv()
+                block = sum_core.at[at[0], at[1]]
+                add(block, [ins[k].at[at[0], at[1], core], from_core.at[at[0], at[1]]])
+                if lag:
+                    group.append(
+                        send(k, block, from_first.at[lag - 1, j], moved(here, axis, lag, dims))
+                    )
+        first.append(group)
+    table_add(1, 0, table_copies, table_sum[1])
+    table_copies = table_step(2, 1, table_sum[1])
+    second = []
+    for k in range(count):
+        axis = k % 2
+        cross = 1 - axis
+        sum_core, from_first, sum_first, from_second = bufs[k][1:5]
+        for copy in first[k]:
+            copy.wait_recv()
+        group = []
+        for lag in list(range(1, dims[cross])) + [0]:
+            at = moved(here, cross, lag, dims)
+            j = at[cross]
+            block = sum_first.at[j]
+            add(
+                block,
+                [sum_core.at[at[0], at[1]]]
+                + [from_first.at[s - 1, j] for s in range(1, dims[axis])],
+            )
+            if lag:
+                group.append(send(k, block, from_second.at[lag - 1], at))
+        second.append(group)
+    table_add(2, 1, table_copies, table_sum[2])
+    table_copies = table_step(3, 3, table_sum[2])
+    third = []
+    for k in range(count):
+        axis = k % 2
+        cross = 1 - axis
+        sum_first, from_second, sum_second, from_third = bufs[k][3:7]
+        for copy in second[k]:
+            copy.wait_recv()
+        add(
+            sum_second,
+            [sum_first.at[here[cross]]] + [from_second.at[s - 1] for s in range(1, dims[cross])],
+        )
+        group = []
+        for step in range(1, depth):
+            at = moved(here, 3, step, dims)
+            group.append(send(k, sum_second.at[at[3]], from_third.at[step - 1], at))
+        third.append(group)
+    table_add(3, 3, table_copies, table_out)
+    for k in range(count):
+        sum_second, from_third = bufs[k][5:7]
+        for copy in third[k]:
+            copy.wait_recv()
+        total = sum_second[z].astype(jnp.float32)
+        for step in range(1, depth):
+            total = total + from_third[step - 1].astype(jnp.float32)
+        outs[k][...] = total
+    for copy in started:
+        copy.wait_send()
+
+
+def sizes_here():
+    rows, depth = lax.axis_size("rows"), lax.axis_size("cols")
+    height, width = grid_of(rows)
+    return height, width, CORES, depth
+
+
+def blocked(rows, columns):
+    if rows % 16 == 0:
+        return rows, columns
+    return rows * columns // 128, 128
+
+
+def gather_all(shards):
+    dims = sizes_here()
+    height, width, cores, depth = dims
+    count = len(shards)
+    blocks = [blocked(*shard.shape) for shard in shards]
+    slots = (depth - 1) + max(height, width) * 2 * height * width
+    outs = pl.pallas_call(
+        functools.partial(gather_kernel, dims, count),
+        name="gather_all",
+        out_shape=[
+            jax.ShapeDtypeStruct(dims + block, shard.dtype)
+            for block, shard in zip(blocks, shards)
+        ],
+        in_specs=[pl.BlockSpec(memory_space=pltpu.VMEM)] * count,
+        out_specs=[pl.BlockSpec(memory_space=pl.ANY)] * count,
+        scratch_shapes=[
+            pltpu.SemaphoreType.DMA((count,)),
+            pltpu.SemaphoreType.DMA((count, slots)),
+            pltpu.SemaphoreType.DMA((count, slots)),
+        ],
+        compiler_params=pltpu.CompilerParams(collective_id=0, has_side_effects=True),
+    )(*[shard.reshape(block) for block, shard in zip(blocks, shards)])
+    total = height * width * cores * depth
+    return [
+        out.reshape(total * shard.shape[0], shard.shape[1]) for out, shard in zip(outs, shards)
+    ]
+
+
+def reduce_all(wholes, table):
+    dims = sizes_here()
+    height, width, cores, depth = dims
+    total = height * width * cores * depth
+    count = len(wholes)
+    shares = [(whole.shape[0] // total, whole.shape[1]) for whole in wholes]
+    blocks = [blocked(*share) for share in shares]
+    scratch = []
+    for k, (block, whole) in enumerate(zip(blocks, wholes)):
+        along, cross = dims[k % 2], dims[1 - k % 2]
+        for lead in (
+            (height, width, depth),
+            (height, width, depth),
+            (max(along - 1, 1), cross, depth),
+            (cross, depth),
+            (max(cross - 1, 1), depth),
+            (depth,),
+            (max(depth - 1, 1),),
+        ):
+            scratch.append(pltpu.VMEM(lead + block, whole.dtype))
+    for size in (cores, height, width, depth):
+        scratch.append(pltpu.VMEM((size,) + table.shape, table.dtype))
+    scratch += [pltpu.VMEM(table.shape, table.dtype)] * 3
+    slots = 2 * height * width + height + width + depth
+    scratch += [pltpu.SemaphoreType.DMA((count + 1, slots))] * 2
+    outs = pl.pallas_call(
+        functools.partial(reduce_kernel, dims, count),
+        name="reduce_all",
+        out_shape=[jax.ShapeDtypeStruct(block, jnp.float32) for block in blocks]
+        + [jax.ShapeDtypeStruct(table.shape, table.dtype)],
+        in_specs=[pl.BlockSpec(memory_space=pltpu.VMEM)] * (count + 1),
+        out_specs=[pl.BlockSpec(memory_space=pltpu.VMEM)] * (count + 1),
+        scratch_shapes=scratch,
+        compiler_params=pltpu.CompilerParams(collective_id=1, has_side_effects=True),
+    )(*[whole.reshape(dims + block) for block, whole in zip(blocks, wholes)], table)
+    return [out.reshape(share) for out, share in zip(outs, shares)], outs[-1]
+
+
+def padded(values, multiple):
+    size = values.shape[-1]
+    extra = -size % multiple
+    return jnp.pad(values, [(0, 0)] * (values.ndim - 1) + [(0, extra)])
 
 
 def per_device(
@@ -113,26 +474,29 @@
     up_bias,
     down_bias,
 ):
-    gathered = (
-        lax.all_gather(qkv_weight, ("rows", "cols"), axis=0, tiled=True),
-        lax.all_gather(proj_weight, ("rows", "cols"), axis=0, tiled=True),
-        lax.all_gather(up_weight, ("rows", "cols"), axis=0, tiled=True),
-        lax.all_gather(down_weight, ("rows", "cols"), axis=0, tiled=True),
-        lax.all_gather(norm1_gain, ("rows", "cols"), axis=0, tiled=True),
-        lax.all_gather(norm1_bias, ("rows", "cols"), axis=0, tiled=True),
-        lax.all_gather(query_bias, ("rows", "cols"), axis=0, tiled=True),
-        lax.all_gather(value_bias, ("rows", "cols"), axis=0, tiled=True),
-        lax.all_gather(proj_bias, ("rows", "cols"), axis=0, tiled=True),
-        lax.all_gather(norm2_gain, ("rows", "cols"), axis=0, tiled=True),
-        lax.all_gather(norm2_bias, ("rows", "cols"), axis=0, tiled=True),
-        lax.all_gather(up_bias, ("rows", "cols"), axis=0, tiled=True),
-        lax.all_gather(down_bias, ("rows", "cols"), axis=0, tiled=True),
-    )
+    shards = (
+        norm1_gain,
+        norm1_bias,
+        query_bias,
+        value_bias,
+        proj_bias,
+        norm2_gain,
+        norm2_bias,
+        up_bias,
+        down_bias,
+    )
+    vector_shard = padded(jnp.concatenate(shards)[None], 2048).reshape(-1, 128)
+    qkv_full, down_full, up_full, proj_full, vector_full = gather_all(
+        [qkv_weight, down_weight, up_weight, proj_weight, vector_shard]
+    )
+    device_count = lax.axis_size("rows") * lax.axis_size("cols")
+    vector_full = vector_full.reshape(device_count, -1)
+    vectors, offset = [], 0
+    for shard in shards:
+        size = shard.shape[0]
+        vectors.append(vector_full[:, offset : offset + size].reshape(device_count * size))
+        offset += size
     (
-        qkv_full,
-        proj_full,
-        up_full,
-        down_full,
         gain_one_full,
         bias_one_full,
         query_add,
@@ -142,7 +506,7 @@
         bias_two_full,
         up_add,
         down_add,
-    ) = gathered
+    ) = vectors
     tokens_tile, grad_tile = roll_in(images, cotangent)
     image_count, tile_side, features = (
         tokens_tile.shape[0],
@@ -215,47 +579,24 @@
     gauss_cdf = 0.5 * (1.0 + lax.erf(hidden_pre * root_half))
     act_b = (hidden_pre * gauss_cdf).astype(jnp.bfloat16)
     result = residual + dot_plain(act_b, down_full) + down_add.astype(jnp.float32)
-    regathered = (
-        lax.all_gather(qkv_weight, ("rows", "cols"), axis=0, tiled=True),
-        lax.all_gather(proj_weight, ("rows", "cols"), axis=0, tiled=True),
-        lax.all_gather(up_weight, ("rows", "cols"), axis=0, tiled=True),
-        lax.all_gather(down_weight, ("rows", "cols"), axis=0, tiled=True),
-        lax.all_gather(norm1_gain, ("rows", "cols"), axis=0, tiled=True),
-        lax.all_gather(norm1_bias, ("rows", "cols"), axis=0, tiled=True),
-        lax.all_gather(query_bias, ("rows", "cols"), axis=0, tiled=True),
-        lax.all_gather(value_bias, ("rows", "cols"), axis=0, tiled=True),
-        lax.all_gather(proj_bias, ("rows", "cols"), axis=0, tiled=True),
-        lax.all_gather(norm2_gain, ("rows", "cols"), axis=0, tiled=True),
-        lax.all_gather(norm2_bias, ("rows", "cols"), axis=0, tiled=True),
-        lax.all_gather(up_bias, ("rows", "cols"), axis=0, tiled=True),
-        lax.all_gather(down_bias, ("rows", "cols"), axis=0, tiled=True),
-    )
-    qkv_back, proj_back, up_back, down_back = (
-        regathered[0],
-        regathered[1],
-        regathered[2],
-        regathered[3],
-    )
-    gain_one_back = regathered[4].astype(jnp.float32)
-    gain_two_back = regathered[9].astype(jnp.float32)
     grad_b = grad_rows.astype(jnp.bfloat16)
     grad_down = dot_lead(act_b, grad_b)
     grad_down_add = jnp.sum(grad_rows, axis=0)
-    grad_act = dot_tail(grad_b, down_back)
+    grad_act = dot_tail(grad_b, down_full)
     density = jnp.exp(-0.5 * hidden_pre * hidden_pre) * tau_factor
     grad_pre = grad_act * (gauss_cdf + hidden_pre * density)
     grad_pre_b = grad_pre.astype(jnp.bfloat16)
     grad_up = dot_lead(h_two, grad_pre_b)
     grad_up_add = jnp.sum(grad_pre, axis=0)
-    grad_h_two = dot_tail(grad_pre_b, up_back)
+    grad_h_two = dot_tail(grad_pre_b, up_full)
     grad_resid, grad_gain_two, grad_bias_two = norm_back(
-        grad_h_two, normed_two, inv_two, gain_two_back
+        grad_h_two, normed_two, inv_two, gain_two
     )
     grad_resid = grad_resid + grad_rows
     grad_resid_b = grad_resid.astype(jnp.bfloat16)
     grad_proj = dot_lead(attn_b, grad_resid_b)
     grad_proj_add = jnp.sum(grad_resid, axis=0)
-    grad_attn_b = dot_tail(grad_resid_b, proj_back).astype(jnp.bfloat16)
+    grad_attn_b = dot_tail(grad_resid_b, proj_full).astype(jnp.bfloat16)
     grad_heads = split_heads(grad_attn_b)
     grad_attend = jnp.einsum(
         "wqhd,wkhd->whqk", grad_heads, split_heads(value_b), preferred_element_type=jnp.float32
@@ -291,27 +632,44 @@
     grad_value_add = jnp.sum(grad_value, axis=0)
     grad_mixed_b = jnp.concatenate([grad_query, grad_key, grad_value], axis=1).astype(jnp.bfloat16)
     grad_qkv = dot_lead(h_one, grad_mixed_b)
-    grad_h_one = dot_tail(grad_mixed_b, qkv_back)
+    grad_h_one = dot_tail(grad_mixed_b, qkv_full)
     grad_in, grad_gain_one, grad_bias_one = norm_back(
-        grad_h_one, normed_one, inv_one, gain_one_back
+        grad_h_one, normed_one, inv_one, gain_one
     )
     grad_tokens = grad_resid + grad_in
-    grad_table = lax.psum(table_local, ("rows", "cols"))
-    shard_grads = (
-        lax.psum_scatter(grad_qkv, ("rows", "cols"), scatter_dimension=0, tiled=True),
-        lax.psum_scatter(grad_proj, ("rows", "cols"), scatter_dimension=0, tiled=True),
-        lax.psum_scatter(grad_up, ("rows", "cols"), scatter_dimension=0, tiled=True),
-        lax.psum_scatter(grad_down, ("rows", "cols"), scatter_dimension=0, tiled=True),
-        lax.psum_scatter(grad_gain_one, ("rows", "cols"), scatter_dimension=0, tiled=True),
-        lax.psum_scatter(grad_bias_one, ("rows", "cols"), scatter_dimension=0, tiled=True),
-        lax.psum_scatter(grad_query_add, ("rows", "cols"), scatter_dimension=0, tiled=True),
-        lax.psum_scatter(grad_value_add, ("rows", "cols"), scatter_dimension=0, tiled=True),
-        lax.psum_scatter(grad_proj_add, ("rows", "cols"), scatter_dimension=0, tiled=True),
-        lax.psum_scatter(grad_gain_two, ("rows", "cols"), scatter_dimension=0, tiled=True),
-        lax.psum_scatter(grad_bias_two, ("rows", "cols"), scatter_dimension=0, tiled=True),
-        lax.psum_scatter(grad_up_add, ("rows", "cols"), scatter_dimension=0, tiled=True),
-        lax.psum_scatter(grad_down_add, ("rows", "cols"), scatter_dimension=0, tiled=True),
-    )
+    vector_grads = (
+        grad_gain_one,
+        grad_bias_one,
+        grad_query_add,
+        grad_value_add,
+        grad_proj_add,
+        grad_gain_two,
+        grad_bias_two,
+        grad_up_add,
+        grad_down_add,
+    )
+    vector_rows = padded(
+        jnp.concatenate([grad.reshape(device_count, -1) for grad in vector_grads], axis=1), 2048
+    ).reshape(-1, 128)
+    table_rows = padded(table_local.reshape(1, -1), 1024).reshape(-1, 128)
+    (down_sum, up_sum, qkv_sum, proj_sum, vector_sum), table_sum = reduce_all(
+        [
+            grad_down.astype(jnp.bfloat16),
+            grad_up.astype(jnp.bfloat16),
+            grad_qkv.astype(jnp.bfloat16),
+            grad_proj.astype(jnp.bfloat16),
+            vector_rows,
+        ],
+        table_rows,
+    )
+    grad_table = table_sum.reshape(-1)[: table_local.size].reshape(table_local.shape)
+    vector_sum = vector_sum.reshape(-1)
+    vector_sums, offset = [], 0
+    for shard in shards:
+        size = shard.shape[0]
+        vector_sums.append(vector_sum[offset : offset + size])
+        offset += size
+    shard_grads = (qkv_sum, proj_sum, up_sum, down_sum, *vector_sums)
     block_out, grad_images = roll_out(
         result.reshape(image_count, tile_side, tile_side, features),
         grad_tokens.reshape(image_count, tile_side, tile_side, features),

time: 751 us -> 210 us (0.28)
  waiting for transfers between devices: 484 us -> 14.3 us
  blocking collectives: 150 us -> 0 us
  Pallas kernels: 0 us -> 103 us
  between operations: 15 us -> 1.63 us
    reduce_scatter x4 -> x0, waiting for transfers between devices: 446 us -> none  [the longest x1 151 us: per_device(): lax.psum_scatter(grad_up, ('rows', 'cols'), scatter_dimension=0, tiled=True)]
    pallas_call x0 -> x2, Pallas kernels: none -> 103 us  [the longest x1 54.6 us: reduce_all(): pl.pallas_call(functools.partial(reduce_kernel, dims, count), name='reduc...]
    unnamed x2 -> x0, blocking collectives: 77.1 us -> none
    all_gather x1 -> x0, blocking collectives: 72.4 us -> none  [per_device(): lax.all_gather(proj_weight, ('rows', 'cols'), axis=0, tiled=True)]
    all_gather x3 -> x0, waiting for transfers between devices: 24.9 us -> none  [the longest x1 24.8 us: per_device(): lax.all_gather(down_weight, ('rows', 'cols'), axis=0, tiled=True)]
    unnamed x135 -> x108, local copies, waits for them, and re-layouts: 16.1 us -> 8.02 us
  transfers between devices with their start and end apart: 15 -> 8, of which waited for: 10 -> 5; matrix products, arithmetic and copies ran while one was open for 9% -> 13% of each run, Pallas kernels for 0% -> 49%
where the time goes in v1:
time: 210 us; the launch traced here: 209 us
  Pallas kernels  103 us (49%)
  local copies, waits for them, and re-layouts  43.5 us (21%)
  matrix products  31.5 us (15%)
  waiting for transfers between devices  14.3 us (7%)
  starting transfers between devices  9.49 us (5%)
  other arithmetic  5.64 us (3%)
    pallas_call x1, Pallas kernels, reduce_all(): pl.pallas_call(functools.partial(reduce_kernel, dims, count), name='reduc...  54.6 us
    pallas_call x1, Pallas kernels, gather_all(): pl.pallas_call(functools.partial(gather_kernel, dims, count), name='gathe...  48.4 us
    ppermute x8, waiting for transfers between devices, shifted(): lax.ppermute(array, axis, [(i, (i + by) % length) for i in range(length)])  14.3 us
    reshape x8, local copies, waits for them, and re-layouts, split_heads(): return values.reshape(image_count, window, head_count, head_width)  10.3 us
    ppermute x8, starting transfers between devices, shifted(): lax.ppermute(array, axis, [(i, (i + by) % length) for i in range(length)])  9.49 us
    unnamed x108, local copies, waits for them, and re-layouts  8.02 us
    dot_general x4, matrix products, dot_lead(): lax.dot_general(former, latter, (((0,), (0,)), ((), ())), preferred_eleme...  7.28 us
    dot_general x4, matrix products, dot_tail(): lax.dot_general(former, latter, (((1,), (1,)), ((), ())), preferred_eleme...  6.44 us
  transfers between devices with their start and end apart: 8, of which 5 were waited for; matrix products, arithmetic and copies ran while one was open for 13% of the time, Pallas kernels for 49%

profile of v1, /device:TPU:0, one launch (start us, length us, event | category | flops | bytes accessed | tf_op | source)
XLA Modules:
  0.0 209.0 jit_solution(564740518731154463)
XLA Ops:
  0.7 1.0 slice.143
  1.7 3.4 %collective-permute-start.4 = (f32[4,3,7,512]{3,0,2,1:T(4,128)S(1)}, f32[4,3,7,512]{3,0,2,1:T(4,128)S(1)}, u32[]{:S(2)}, u32[]{:S(2)}) collective-permute-start(f32[4,3,7,512]{3,0,2,1:T(4,128)S(1)} %slice.143), channel_id=1, source_target_pairs={{0,28},{4,0},{8,4},{12,8},{16,12},{20,16},{24,20},{28,24},{1,29},{... | collective-permute-start | bytes 516104 | tf_op jit(solution)/shard_map/ppermute | solution.py:22
  5.1 0.9 slice.123
  6.0 0.7 collective-permute-start
  6.8 6.1 %concatenate.36 = bf16[192]{0:T(256)(128)(2,1)S(1)} concatenate(bf16[16]{0:T(256)(128)(2,1)} %param.25, bf16[16]{0:T(256)(128)(2,1)} %param.26, bf16[16]{0:T(256)(128)(2,1)} %param.27, bf16[16]{0:T(256)(128)(2,1)} %param.28, bf16[16]{0:T(256)(128)(2,1)} %param.29, bf16[16]{0:T(256)(128)(2,1)} %param.30, bf16[16]{0:T(256)(128)(2,1)} %param.31, bf16[64]{0:T(256)(128)(2,1)} %param.32, ...), dimensions={0} | concatenate | bytes 768 | tf_op jit(solution)/shard_map/concatenate | solution.py:488
  13.5 48.4 %gather_all.1 = (bf16[2,2,2,4,16,1536]{5,4,3,2,1,0:T(8,128)(2,1)}, bf16[2,2,2,4,64,512]{5,4,3,2,1,0:T(8,128)(2,1)}, bf16[2,2,2,4,16,2048]{5,4,3,2,1,0:T(8,128)(2...) custom-call(bf16[16,1536]{1,0:T(8,128)(2,1)} %refs_0_.1, bf16[64,512]{1,0:T(8,128)(2,1)} %refs_1_.1, ...), custom_call_target="tpu_custom_call" | custom-call | tf_op jit(solution)/shard_map/gather_all/pallas_call | solution.py:392
  61.9 0.9 copy.132
  63.2 0.9 eq.35
  64.1 1.2 convolution_bitcast_fusion
  65.7 1.0 copy.91
  70.4 3.4 %collective-permute-start.1 = (f32[4,7,3,512]{3,0,2,1:T(4,128)S(1)}, f32[4,7,3,512]{3,0,2,1:T(4,128)S(1)}, u32[]{:S(2)}, u32[]{:S(2)}) collective-permute-start(f32[4,7,3,512]{3,0,2,1:T(4,128)S(1)} %pad_maximum_fusion.5), channel_id=1, source_target_pairs={{0,3},{1,0},{2,1},{3,2},{4,7},{5,4},{6,5},{7,6},{8,11},{9,8},{10,9... | collective-permute-start | bytes 516104 | tf_op jit(solution)/shard_map/ppermute | solution.py:22
  74.8 3.7 %collective-permute-done.1 = f32[4,7,3,512]{3,0,2,1:T(4,128)S(1)} collective-permute-done((f32[4,7,3,512]{3,0,2,1:T(4,128)S(1)}, f32[4,7,3,512]{3,0,2,1:T(4,128)S(1)}, u32[]{:S(2)}, u32[]{:S(2)}) %collective-permute-start.1) | collective-permute-done | bytes 172064 | tf_op jit(solution)/shard_map/ppermute | solution.py:22
  79.3 2.4 %collective-permute-done.5 = f32[4,7,3,512]{3,0,2,1:T(4,128)S(1)} collective-permute-done((f32[4,7,3,512]{3,0,2,1:T(4,128)S(1)}, f32[4,7,3,512]{3,0,2,1:T(4,128)S(1)}, u32[]{:S(2)}, u32[]{:S(2)}) %collective-permute-start.5) | collective-permute-done | bytes 172064 | tf_op jit(solution)/shard_map/ppermute | solution.py:22
  81.9 0.8 convert_element_type.257
  83.6 0.8 copy-done.13
  85.5 1.5 copy.89
  87.5 1.6 copy.90
  89.5 0.7 copy.92
  90.2 2.2 %fusion.52 = (f32[4,16,49]{2,1,0:T(8,128)S(1)}, f32[4,16,49,49]{2,3,1,0:T(8,128)S(1)}) fusion(f32[16,49,49]{1,2,0:T(8,128)} %copy.91, bf16[4,49,16,32]{1,3,2,0:T(8,128)(2,1)} %copy.89, bf16[4,49,16,32]{1,3,2,0:T(8,128)(2,1)} %copy.90, pred[49,49]{0,1:T(8,128)(4,1)S(1)} %broadcast_compare_fusion), kind=kOutput, calls=%fused_computation.135 | convolution fusion | flops 10292352 | bytes 1184673 | tf_op jit(solution)/shard_map/wqhd,wkhd->whqk/dot_general | solution.py:546
  94.1 1.5 fusion.53
  95.9 3.6 %multiply_convert_fusion = (bf16[196,2048]{1,0:T(8,128)(2,1)}, f32[196,2048]{1,0:T(8,128)S(1)}) fusion(f32[2048]{0:T(1024)} %reshape.502, bf16[512,2048]{1,0:T(8,128)(2,1)} %bitcast.71, f32[196,512]{1,0:T(8,128)S(1)} %get-tuple-element.111, f32[512]{0:T(512)} %reshape.501, f32[512]{0:T(512)} %reshape.500, f32[196]{0:T(256)S(1)} %add_rsqrt_fusion.1, ...), kind=kOutput, calls=%fused_computation.18 | convolution fusion | flops 413952000 | bytes 4920864 | tf_op jit(solution)/shard_map/dot_general | solution.py:52
  99.5 1.7 fusion.54
  101.2 1.5 multiply_reduce_fusion.1
  102.7 0.7 fusion.48
  103.5 1.0 convolution_convert_fusion.6
  104.5 1.1 convolution_convert_fusion.3
  105.6 2.3 %reshape.507 = bf16[4,49,16,32]{3,2,1,0:T(8,128)(2,1)} reshape(bf16[196,512]{1,0:T(8,128)(2,1)} %convolution_convert_fusion.6) | data formatting | bytes 401408 | tf_op jit(solution)/shard_map/reshape | solution.py:543
  107.9 2.8 %copy.99 = bf16[4,49,16,32]{1,3,2,0:T(8,128)(2,1)} copy(bf16[4,49,16,32]{3,2,1,0:T(8,128)(2,1)} %reshape.507) | data formatting | bytes 401408 | tf_op jit(solution)/shard_map/reshape | solution.py:543
  110.7 3.1 %fusion.49 = (f32[16,32]{1,0:T(8,128)}, bf16[4,49,16,32]{1,3,2,0:T(8,128)(2,1)}) fusion(bf16[4,49,16,32]{1,3,2,0:T(8,128)(2,1)} %copy.99, f32[4,16,49,49]{2,3,1,0:T(8,128)S(1)} %get-tuple-element.109, f32[4,16,49]{2,1,0:T(8,128)S(1)} %log_add_fusion), kind=kOutput, calls=%fused_computation.132 | convolution fusion | flops 10342016 | bytes 1030656 | tf_op jit(solution)/shard_map/whqk,wqhd->wkhd/dot_general | solution.py:605
  113.8 0.7 multiply_reduce_fusion
  114.5 1.4 fusion.45
  116.0 1.4 fusion.8
  118.8 1.5 copy.106
  121.4 2.3 %multiply_reduce_fusion.2 = (f32[512]{0:T(512)S(1)}, f32[196]{0:T(256)S(1)}, f32[196]{0:T(256)S(1)}, f32[512]{0:T(512)S(1)}, f32[196,512]{1,0:T(8,128)S(1)}) fusion(f32[196,512]{1,0:T(8,128)S(1)} %reshape.463, f32[196]{0:T(256)S(1)} %div.33, f32[196]{0:T(256)S(1)} %rsqrt.22, f32[512]{0:T(512)S(1)} %copy-done.25, ...), kind=kOutput, calls=%fused_computation.54 | convolution fusion | flops 309183104 | bytes 2987072 | tf_op jit(solution)/shard_map/dot_general | solution.py:62
  123.7 1.9 convolution_convert_fusion.2
  125.7 2.2 %convolution_convert_fusion = bf16[512,2048]{1,0:T(8,128)(2,1)} fusion(bf16[196,2048]{1,0:T(8,128)(2,1)S(1)} %copy-done.17, f32[196,512]{1,0:T(8,128)S(1)} %get-tuple-element.111, f32[512]{0:T(512)S(1)} %copy-done.34, f32[512]{0:T(512)S(1)} %copy-done.29, f32[196]{0:T(256)S(1)} %copy-done.36, f32[196]{0:T(256)S(1)} %copy-done.31), kind=kOutput, calls=%fused_computation.1 | convolution fusion | flops 412592128 | bytes 3307040 | tf_op jit(solution)/shard_map/dot_general | solution.py:56
  128.0 2.1 convolution_convert_fusion.1
  132.1 1.9 fusion.9
  135.1 0.8 copy.130
  136.0 54.6 %reduce_all.1 = (f32[64,512]{1,0:T(8,128)}, f32[16,2048]{1,0:T(8,128)}, f32[16,1536]{1,0:T(8,128)}, f32[16,512]{1,0:T(8,128)}, f32[16,128]{1,0:T(8,128)}, /*index=5*/f32[24,128]{1,0:T(8,128)}) custom-call(bf16[2,2,2,4,64,512]{5,4,3,2,1,0:T(8,128)(2,1)} %bitcast.69, bf16[2,2,2,4,16,2048]{5,4,3,2,1,0:T(8,128)(2,1)} %bitcast.68, ...), custom_call_target="tpu_custom_call" | custom-call | tf_op jit(solution)/shard_map/reduce_all/pallas_call | solution.py:439
  190.6 1.6 fusion.51
  192.3 1.3 slice.192
  194.5 0.7 collective-permute-start.3
  195.2 3.3 %collective-permute-done.6 = bf16[4,3,7,512]{3,2,1,0:T(8,128)(2,1)S(1)} collective-permute-done((bf16[4,3,7,512]{3,2,1,0:T(8,128)(2,1)S(1)}, bf16[4,3,7,512]{3,2,1,0:T(8,128)(2,1)S(1)}, u32[]{:S(2)}, u32[]{:S(2)}) %collective-permute-start.6) | collective-permute-done | bytes 86048 | tf_op jit(solution)/shard_map/ppermute | solution.py:22
  199.4 2.4 %collective-permute-done.3 = bf16[4,7,3,512]{3,2,1,0:T(4,128)(2,1)S(1)} collective-permute-done((bf16[4,7,3,512]{3,2,1,0:T(4,128)(2,1)S(1)}, bf16[4,7,3,512]{3,2,1,0:T(4,128)(2,1)S(1)}, u32[]{:S(2)}, u32[]{:S(2)}) %collective-permute-start.3) | collective-permute-done | bytes 86048 | tf_op jit(solution)/shard_map/ppermute | solution.py:22
  201.9 1.0 copy.113
  202.9 2.4 %collective-permute-done.7 = bf16[4,7,3,512]{3,2,1,0:T(4,128)(2,1)S(1)} collective-permute-done((bf16[4,7,3,512]{3,2,1,0:T(4,128)(2,1)S(1)}, bf16[4,7,3,512]{3,2,1,0:T(4,128)(2,1)S(1)}, u32[]{:S(2)}, u32[]{:S(2)}) %collective-permute-start.7) | collective-permute-done | bytes 86048 | tf_op jit(solution)/shard_map/ppermute | solution.py:22
  205.4 1.0 copy.114
  (211 shorter events, 21.9 us)
Async XLA Ops:
  0.6 63.4 %copy-start = (f32[169,16]{0,1:T(8,128)S(1)}, f32[169,16]{0,1:T(8,128)}, u32[]{:S(2)}) copy-start(f32[169,16]{0,1:T(8,128)} %param.20) | copy-start | bytes 32452
  0.7 64.8 %copy-start.19 = (f32[4,7,7,512]{3,0,2,1:T(4,128)S(1)}, f32[4,7,7,512]{3,0,2,1:T(4,128)}, u32[]{:S(2)}) copy-start(f32[4,7,7,512]{3,0,2,1:T(4,128)} %param.18) | copy-start | bytes 1204228
  0.7 64.8 %copy-start.18 = (f32[4,7,7,512]{3,0,2,1:T(4,128)S(1)}, f32[4,7,7,512]{3,0,2,1:T(4,128)}, u32[]{:S(2)}) copy-start(f32[4,7,7,512]{3,0,2,1:T(4,128)} %param.17) | copy-start | bytes 1204228
  1.7 72.1 %collective-permute-start.4 = (f32[4,3,7,512]{3,0,2,1:T(4,128)S(1)}, f32[4,3,7,512]{3,0,2,1:T(4,128)S(1)}, u32[]{:S(2)}, u32[]{:S(2)}) collective-permute-start(f32[4,3,7,512]{3,0,2,1:T(4,128)S(1)} %slice.143), channel_id=1, source_target_pairs={{0,28},{4,0},{8,4},{12,8},{16,12},{20,16},{24,20},{28,24},{1,29},{... | collective-permute-start | bytes 516104 | tf_op jit(solution)/shard_map/ppermute | solution.py:22
  6.0 64.3 %collective-permute-start = (f32[4,3,7,512]{3,0,2,1:T(4,128)S(1)}, f32[4,3,7,512]{3,0,2,1:T(4,128)S(1)}, u32[]{:S(2)}, u32[]{:S(2)}) collective-permute-start(f32[4,3,7,512]{3,0,2,1:T(4,128)S(1)} %slice.123), channel_id=1, source_target_pairs={{0,28},{4,0},{8,4},{12,8},{16,12},{20,16},{24,20},{28,24},{1,29},{... | collective-permute-start | bytes 516104 | tf_op jit(solution)/shard_map/ppermute | solution.py:22
  68.8 14.2 %copy-start.24 = (f32[512]{0:T(512)}, f32[512]{0:T(512)S(1)}, u32[]{:S(2)}) copy-start(f32[512]{0:T(512)S(1)} %reshape.495) | copy-start | bytes 6148
  69.5 13.4 %copy-start.32 = (f32[512]{0:T(512)}, f32[512]{0:T(512)S(1)}, u32[]{:S(2)}) copy-start(f32[512]{0:T(512)S(1)} %reshape.496) | copy-start | bytes 6148
  70.4 8.1 %collective-permute-start.1 = (f32[4,7,3,512]{3,0,2,1:T(4,128)S(1)}, f32[4,7,3,512]{3,0,2,1:T(4,128)S(1)}, u32[]{:S(2)}, u32[]{:S(2)}) collective-permute-start(f32[4,7,3,512]{3,0,2,1:T(4,128)S(1)} %pad_maximum_fusion.5), channel_id=1, source_target_pairs={{0,3},{1,0},{2,1},{3,2},{4,7},{5,4},{6,5},{7,6},{8,11},{9,8},{10,9... | collective-permute-start | bytes 516104 | tf_op jit(solution)/shard_map/ppermute | solution.py:22
  73.8 7.9 %collective-permute-start.5 = (f32[4,7,3,512]{3,0,2,1:T(4,128)S(1)}, f32[4,7,3,512]{3,0,2,1:T(4,128)S(1)}, u32[]{:S(2)}, u32[]{:S(2)}) collective-permute-start(f32[4,7,3,512]{3,0,2,1:T(4,128)S(1)} %pad_maximum_fusion.4), channel_id=1, source_target_pairs={{0,3},{1,0},{2,1},{3,2},{4,7},{5,4},{6,5},{7,6},{8,11},{9,8},{10,9... | collective-permute-start | bytes 516104 | tf_op jit(solution)/shard_map/ppermute | solution.py:22
  83.0 1.4 copy-start.13
  90.2 2.7 %copy-start.1 = (bf16[4,49,16,32]{1,3,2,0:T(8,128)(2,1)}, bf16[4,49,16,32]{1,3,2,0:T(8,128)(2,1)S(1)}, u32[]{:S(2)}) copy-start(bf16[4,49,16,32]{1,3,2,0:T(8,128)(2,1)S(1)} %copy.92) | copy-start | bytes 602116
  94.1 5.4 %copy-start.7 = (bf16[196,512]{0,1:T(8,128)(2,1)}, bf16[196,512]{0,1:T(8,128)(2,1)S(1)}, u32[]{:S(2)}) copy-start(bf16[196,512]{0,1:T(8,128)(2,1)S(1)} %convert_element_type.241) | copy-start | bytes 602116
  95.6 7.1 %copy-start.30 = (f32[196]{0:T(256)}, f32[196]{0:T(256)S(1)}, u32[]{:S(2)}) copy-start(f32[196]{0:T(256)S(1)} %broadcast_multiply_fusion.5) | copy-start | bytes 2356
  95.9 6.9 %copy-start.35 = (f32[196]{0:T(256)}, f32[196]{0:T(256)S(1)}, u32[]{:S(2)}) copy-start(f32[196]{0:T(256)S(1)} %add_rsqrt_fusion.1) | copy-start | bytes 2356
  95.9 3.6 %copy-start.20 = (bf16[196,512]{1,0:T(8,128)(2,1)S(1)}, bf16[196,512]{1,0:T(8,128)(2,1)}, u32[]{:S(2)}) copy-start(bf16[196,512]{1,0:T(8,128)(2,1)} %convert_element_type.257) | copy-start | bytes 602116
  95.9 3.6 %copy-start.46 = (bf16[2,2,2,4,64,512]{5,4,3,2,1,0:T(8,128)(2,1)S(1)}, bf16[2,2,2,4,64,512]{5,4,3,2,1,0:T(8,128)(2,1)}, u32[]{:S(2)}) copy-start(bf16[2,2,2,4,64,512]{5,4,3,2,1,0:T(8,128)(2,1)} %get-tuple-element.31) | copy-start | bytes 6291460
  99.5 1.7 copy-start.9
  99.5 1.7 copy-start.28
  101.2 1.5 copy-start.16
  101.2 2.2 %copy-start.10 = (bf16[2,2,2,4,16,512]{5,4,3,2,1,0:T(8,128)(2,1)S(1)}, bf16[2,2,2,4,16,512]{5,4,3,2,1,0:T(8,128)(2,1)}, u32[]{:S(2)}) copy-start(bf16[2,2,2,4,16,512]{5,4,3,2,1,0:T(8,128)(2,1)} %get-tuple-element.29) | copy-start | bytes 1572868
  102.7 1.8 copy-start.8
  110.7 3.1 %copy-start.2 = (bf16[4,49,16,32]{1,3,2,0:T(8,128)(2,1)S(1)}, bf16[4,49,16,32]{1,3,2,0:T(8,128)(2,1)}, u32[]{:S(2)}) copy-start(bf16[4,49,16,32]{1,3,2,0:T(8,128)(2,1)} %copy-done.1) | copy-start | bytes 602116
  110.7 3.1 %copy-start.3 = (bf16[4,49,16,32]{1,3,2,0:T(8,128)(2,1)S(1)}, bf16[4,49,16,32]{1,3,2,0:T(8,128)(2,1)}, u32[]{:S(2)}) copy-start(bf16[4,49,16,32]{1,3,2,0:T(8,128)(2,1)} %copy.99) | copy-start | bytes 602116
  114.5 1.4 copy-start.4
  116.0 1.4 copy-start.5
  116.0 2.1 %copy-start.11 = (bf16[4,49,16,32]{1,3,2,0:T(8,128)(2,1)S(1)}, bf16[4,49,16,32]{1,3,2,0:T(8,128)(2,1)}, u32[]{:S(2)}) copy-start(bf16[4,49,16,32]{1,3,2,0:T(8,128)(2,1)} %get-tuple-element.87) | copy-start | bytes 602116
  121.4 2.3 %copy-start.33 = (f32[512]{0:T(512)S(1)}, f32[512]{0:T(512)}, u32[]{:S(2)}) copy-start(f32[512]{0:T(512)} %copy-done.32) | copy-start | bytes 6148
  123.7 2.0 copy-start.17
  123.7 2.0 copy-start.29
  123.7 1.9 copy-start.31
  123.7 1.9 copy-start.34
  123.7 1.9 copy-start.36
  125.6 2.2 %copy-start.15 = (f32[4,7,3,512]{3,0,2,1:T(4,128)S(1)}, f32[4,7,3,512]{3,0,2,1:T(4,128)}, u32[]{:S(2)}) copy-start(f32[4,7,3,512]{3,0,2,1:T(4,128)} %copy-done.14) | copy-start | bytes 516100
  125.7 2.3 %copy-start.40 = (f32[512]{0:T(512)S(1)}, f32[512]{0:T(512)}, u32[]{:S(2)}) copy-start(f32[512]{0:T(512)} %get-tuple-element.80) | copy-start | bytes 6148
  125.7 2.4 %copy-start.6 = (bf16[196,2048]{1,0:T(8,128)(2,1)S(1)}, bf16[196,2048]{1,0:T(8,128)(2,1)}, u32[]{:S(2)}) copy-start(bf16[196,2048]{1,0:T(8,128)(2,1)} %get-tuple-element.115) | copy-start | bytes 2408452
  127.9 2.2 %copy-start.43 = (f32[512]{0:T(512)S(1)}, f32[512]{0:T(512)}, u32[]{:S(2)}) copy-start(f32[512]{0:T(512)} %reshape.503) | copy-start | bytes 6148
  128.0 2.1 %copy-start.47 = (bf16[2,2,2,4,64,512]{5,4,3,2,1,0:T(8,128)(2,1)S(1)}, bf16[2,2,2,4,64,512]{5,4,3,2,1,0:T(8,128)(2,1)}, u32[]{:S(2)}) copy-start(bf16[2,2,2,4,64,512]{5,4,3,2,1,0:T(8,128)(2,1)} %get-tuple-element.31) | copy-start | bytes 6291460
  130.1 1.4 copy-start.26
  130.2 1.5 copy-start.12
  131.2 63.2 %collective-permute-start.2 = (bf16[4,3,7,512]{3,2,1,0:T(8,128)(2,1)S(1)}, bf16[4,3,7,512]{3,2,1,0:T(8,128)(2,1)S(1)}, u32[]{:S(2)}, u32[]{:S(2)}) collective-permute-start(bf16[4,3,7,512]{3,2,1,0:T(8,128)(2,1)S(1)} %slice.245), channel_id=1, source_target_pairs={{0,4},{4,8},{8,12},{12,16},{16,20},{20,24},{24,28},{28,0},{1,5},{5... | collective-permute-start | bytes 258056 | tf_op jit(solution)/shard_map/ppermute | solution.py:22
  190.6 3.0 %copy-start.37 = (f32[24,128]{1,0:T(8,128)S(1)}, f32[24,128]{1,0:T(8,128)}, u32[]{:S(2)}) copy-start(f32[24,128]{1,0:T(8,128)} %get-tuple-element.37) | copy-start | bytes 36868
  193.6 4.9 %collective-permute-start.6 = (bf16[4,3,7,512]{3,2,1,0:T(8,128)(2,1)S(1)}, bf16[4,3,7,512]{3,2,1,0:T(8,128)(2,1)S(1)}, u32[]{:S(2)}, u32[]{:S(2)}) collective-permute-start(bf16[4,3,7,512]{3,2,1,0:T(8,128)(2,1)S(1)} %slice.244), channel_id=1, source_target_pairs={{0,4},{4,8},{8,12},{12,16},{16,20},{20,24},{24,28},{28,0},{1,5},{5... | collective-permute-start | bytes 258056 | tf_op jit(solution)/shard_map/ppermute | solution.py:22
  194.5 7.2 %collective-permute-start.3 = (bf16[4,7,3,512]{3,2,1,0:T(4,128)(2,1)S(1)}, bf16[4,7,3,512]{3,2,1,0:T(4,128)(2,1)S(1)}, u32[]{:S(2)}, u32[]{:S(2)}) collective-permute-start(bf16[4,7,3,512]{3,2,1,0:T(4,128)(2,1)S(1)} %fusion.30), channel_id=1, source_target_pairs={{0,1},{1,2},{2,3},{3,0},{4,5},{5,6},{6,7},{7,4},{8,9},{9,10},{10,1... | collective-permute-start | bytes 258056 | tf_op jit(solution)/shard_map/ppermute | solution.py:22
  198.7 6.6 %collective-permute-start.7 = (bf16[4,7,3,512]{3,2,1,0:T(4,128)(2,1)S(1)}, bf16[4,7,3,512]{3,2,1,0:T(4,128)(2,1)S(1)}, u32[]{:S(2)}, u32[]{:S(2)}) collective-permute-start(bf16[4,7,3,512]{3,2,1,0:T(4,128)(2,1)S(1)} %fusion.28), channel_id=1, source_target_pairs={{0,1},{1,2},{2,3},{3,0},{4,5},{5,6},{6,7},{7,4},{8,9},{9,10},{10,1... | collective-permute-start | bytes 258056 | tf_op jit(solution)/shard_map/ppermute | solution.py:22
  201.9 4.6 %copy-start.23 = (f32[16,1536]{1,0:T(8,128)S(1)}, f32[16,1536]{1,0:T(8,128)}, u32[]{:S(2)}) copy-start(f32[16,1536]{1,0:T(8,128)} %get-tuple-element.146) | copy-start | bytes 294916
  201.9 5.2 %copy-start.27 = (f32[16,512]{1,0:T(8,128)S(1)}, f32[16,512]{1,0:T(8,128)}, u32[]{:S(2)}) copy-start(f32[16,512]{1,0:T(8,128)} %get-tuple-element.147) | copy-start | bytes 98308
  201.9 5.8 %copy-start.22 = (f32[16,2048]{1,0:T(8,128)S(1)}, f32[16,2048]{1,0:T(8,128)}, u32[]{:S(2)}) copy-start(f32[16,2048]{1,0:T(8,128)} %get-tuple-element.148) | copy-start | bytes 393220
  201.9 6.5 %copy-start.21 = (f32[64,512]{1,0:T(8,128)S(1)}, f32[64,512]{1,0:T(8,128)}, u32[]{:S(2)}) copy-start(f32[64,512]{1,0:T(8,128)} %get-tuple-element.149) | copy-start | bytes 393220
  (8 other events, 7.6 us)

commit v2 on v1

--- a/solution.py
+++ b/solution.py
@@ -7,6 +7,7 @@
 from jax.experimental.pallas import tpu as pltpu
 from jax.sharding import PartitionSpec as P
 
+
 WIN = 7
 SHIFT = 3
 
@@ -20,14 +21,6 @@
 def shifted(array, axis, by):
     length = lax.axis_size(axis)
     return lax.ppermute(array, axis, [(i, (i + by) % length) for i in range(length)])
-
-
-def as_sent(array):
-
-    def short(part):
-        return part.astype(jnp.bfloat16) if part.dtype == jnp.float32 else part
-
-    return jax.tree.map(short, array)
 
 
 def layer_norm(values, gain_vec, offset):
@@ -70,32 +63,35 @@
     )
 
 
-def roll_in(images, cotangent):
-    from_below = shifted((images[:, :SHIFT], cotangent[:, :SHIFT]), "rows", -1)
-    tall_tokens = jnp.concatenate([images[:, SHIFT:], from_below[0]], axis=1)
-    tall_grads = jnp.concatenate([cotangent[:, SHIFT:], from_below[1]], axis=1)
-    beside = shifted((tall_tokens[:, :, :SHIFT], tall_grads[:, :, :SHIFT]), "cols", -1)
-    return (
-        jnp.concatenate([tall_tokens[:, :, SHIFT:], beside[0]], axis=2),
-        jnp.concatenate([tall_grads[:, :, SHIFT:], beside[1]], axis=2),
-    )
-
-
-def roll_out(result, grad_tokens):
-    from_above = (
-        shifted(result[:, -SHIFT:].astype(jnp.bfloat16), "rows", 1).astype(jnp.float32),
-        shifted(grad_tokens[:, -SHIFT:].astype(jnp.bfloat16), "rows", 1).astype(jnp.float32),
-    )
-    tall_result = jnp.concatenate([from_above[0], result[:, :-SHIFT]], axis=1)
-    tall_grads = jnp.concatenate([from_above[1], grad_tokens[:, :-SHIFT]], axis=1)
-    beside = (
-        shifted(tall_result[:, :, -SHIFT:].astype(jnp.bfloat16), "cols", 1).astype(jnp.float32),
-        shifted(as_sent(tall_grads[:, :, -SHIFT:]), "cols", 1),
-    )
-    return (
-        jnp.concatenate([beside[0], tall_result[:, :, :-SHIFT]], axis=2),
-        jnp.concatenate([beside[1], tall_grads[:, :, :-SHIFT]], axis=2),
-    )
+def shifted_both(array, by):
+    rows, cols = lax.axis_size("rows"), lax.axis_size("cols")
+    pairs = [
+        (i * cols + j, (i + by) % rows * cols + (j + by) % cols)
+        for i in range(rows)
+        for j in range(cols)
+    ]
+    return lax.ppermute(array, ("rows", "cols"), pairs)
+
+
+def roll_in(both):
+    below = shifted(both[:, :SHIFT, SHIFT:], "rows", -1)
+    beside = shifted(both[:, SHIFT:, :SHIFT], "cols", -1)
+    corner = shifted_both(both[:, :SHIFT, :SHIFT], -1)
+    top = jnp.concatenate([both[:, SHIFT:, SHIFT:], beside], axis=2)
+    bottom = jnp.concatenate([below, corner], axis=2)
+    return jnp.concatenate([top, bottom], axis=1)
+
+
+def roll_out(values):
+    short = values.astype(jnp.bfloat16)
+    above = shifted(short[:, -SHIFT:, :-SHIFT], "rows", 1)
+    beside = shifted(short[:, :-SHIFT, -SHIFT:], "cols", 1)
+    corner = shifted_both(short[:, -SHIFT:, -SHIFT:], 1)
+    top = jnp.concatenate([corner, above], axis=2).astype(jnp.float32)
+    bottom = jnp.concatenate(
+        [beside.astype(jnp.float32), values[:, :-SHIFT, :-SHIFT]], axis=2
+    )
+    return jnp.concatenate([top, bottom], axis=1)
 
 
 MESH = pl.DeviceIdType.MESH
@@ -112,7 +108,7 @@
 
 
 def whereabouts(dims):
-    height, width = dims[0], dims[1]
+    width = dims[1]
     row, depth_at = lax.axis_index("rows"), lax.axis_index("cols")
     core = lax.rem(row, CORES)
     chip = row // CORES
@@ -146,7 +142,7 @@
 def gather_kernel(dims, count, *refs):
     ins, outs = refs[:count], refs[count : 2 * count]
     local_sem, send_sem, recv_sem = refs[2 * count :]
-    height, width, _, depth = dims
+    _, _, _, depth = dims
     here = whereabouts(dims)
     y, x, core, z = here
     greet(dims, here)
@@ -236,9 +232,9 @@
     table_in = rest[7 * count : 7 * count + 4]
     table_sum = rest[7 * count + 4 : 7 * count + 7]
     send_sem, recv_sem = rest[7 * count + 7 :]
-    height, width, _, depth = dims
+    _, _, _, depth = dims
     here = whereabouts(dims)
-    y, x, core, z = here
+    _, _, core, z = here
     greet(dims, here)
     used = [0] * (count + 1)
     started = []
@@ -404,6 +400,7 @@
             pltpu.SemaphoreType.DMA((count, slots)),
         ],
         compiler_params=pltpu.CompilerParams(collective_id=0, has_side_effects=True),
+        cost_estimate=pl.CostEstimate(flops=0, bytes_accessed=150_000_000, transcendentals=0),
     )(*[shard.reshape(block) for block, shard in zip(blocks, shards)])
     total = height * width * cores * depth
     return [
@@ -445,6 +442,7 @@
         out_specs=[pl.BlockSpec(memory_space=pltpu.VMEM)] * (count + 1),
         scratch_shapes=scratch,
         compiler_params=pltpu.CompilerParams(collective_id=1, has_side_effects=True),
+        cost_estimate=pl.CostEstimate(flops=0, bytes_accessed=150_000_000, transcendentals=0),
     )(*[whole.reshape(dims + block) for block, whole in zip(blocks, wholes)], table)
     return [out.reshape(share) for out, share in zip(outs, shares)], outs[-1]
 
@@ -453,6 +451,18 @@
     size = values.shape[-1]
     extra = -size % multiple
     return jnp.pad(values, [(0, 0)] * (values.ndim - 1) + [(0, extra)])
+
+
+def joined(parts):
+    size = sum(part.shape[0] for part in parts)
+    size += -size % 2048
+    total, offset = None, 0
+    for part in parts:
+        after = size - offset - part.shape[0]
+        placed = lax.pad(part.astype(jnp.float32), jnp.float32(0), [(offset, after, 0)])
+        total = placed if total is None else total + placed
+        offset += part.shape[0]
+    return total
 
 
 def per_device(
@@ -485,7 +495,7 @@
         up_bias,
         down_bias,
     )
-    vector_shard = padded(jnp.concatenate(shards)[None], 2048).reshape(-1, 128)
+    vector_shard = joined(shards).astype(jnp.bfloat16).reshape(-1, 128)
     qkv_full, down_full, up_full, proj_full, vector_full = gather_all(
         [qkv_weight, down_weight, up_weight, proj_weight, vector_shard]
     )
@@ -507,7 +517,7 @@
         up_add,
         down_add,
     ) = vectors
-    tokens_tile, grad_tile = roll_in(images, cotangent)
+    tokens_tile, grad_tile = roll_in(images), roll_in(cotangent)
     image_count, tile_side, features = (
         tokens_tile.shape[0],
         tokens_tile.shape[1],
@@ -651,6 +661,9 @@
     vector_rows = padded(
         jnp.concatenate([grad.reshape(device_count, -1) for grad in vector_grads], axis=1), 2048
     ).reshape(-1, 128)
+    block_out = roll_out(result.reshape(image_count, tile_side, tile_side, features))
+    grad_tokens, table_local = lax.optimization_barrier((grad_tokens, table_local))
+    grad_images = roll_out(grad_tokens.reshape(image_count, tile_side, tile_side, features))
     table_rows = padded(table_local.reshape(1, -1), 1024).reshape(-1, 128)
     (down_sum, up_sum, qkv_sum, proj_sum, vector_sum), table_sum = reduce_all(
         [
@@ -670,10 +683,6 @@
         vector_sums.append(vector_sum[offset : offset + size])
         offset += size
     shard_grads = (qkv_sum, proj_sum, up_sum, down_sum, *vector_sums)
-    block_out, grad_images = roll_out(
-        result.reshape(image_count, tile_side, tile_side, features),
-        grad_tokens.reshape(image_count, tile_side, tile_side, features),
-    )
     return (
         block_out,
         grad_images,

time: 210 us -> 223 us (1.062)
  waiting for transfers between devices: 14.3 us -> 3.45 us
  other arithmetic: 5.64 us -> 14.4 us
  starting transfers between devices: 9.49 us -> 16.5 us
  local copies, waits for them, and re-layouts: 43.5 us -> 50.2 us
    ppermute x8, waiting for transfers between devices: 14.3 us -> 3.44 us  [shifted(): lax.ppermute(array, axis, [(i, (i + by) % length) for i in range(length)])]
    slice x8 -> x15, local copies, waits for them, and re-layouts: 2.03 us -> 10.7 us  [the longest x2 2.44 us: roll_in(): beside = shifted(both[:, SHIFT:, :SHIFT], 'cols', -1)]
    ppermute x0 -> x4, starting transfers between devices: none -> 7.24 us  [shifted_both(): return lax.ppermute(array, ('rows', 'cols'), pairs)]
    concatenate x3 -> x2, local copies, waits for them, and re-layouts: 6.4 us -> 1.07 us  [roll_in(): return jnp.concatenate([top, bottom], axis=1)]
    reduce_sum x3 -> x5, other arithmetic: 0.71 us -> 4.64 us  [per_device(): grad_down_add = jnp.sum(grad_rows, axis=0)]
    dot_general x4, matrix products: 6.44 us -> 9.27 us  [dot_tail(): lax.dot_general(former, latter, (((1,), (1,)), ((), ())), preferred_eleme...]
    unnamed x108 -> x136, local copies, waits for them, and re-layouts: 8.02 us -> 8.4 us
  transfers between devices with their start and end apart: 8 -> 12, of which waited for: 5 -> 1; matrix products, arithmetic and copies ran while one was open for 13% -> 23% of each run, Pallas kernels for 49% -> 46%
where the time goes in v2:
time: 223 us; the launch traced here: 222 us
  Pallas kernels  102 us (46%)
  local copies, waits for them, and re-layouts  50.2 us (23%)
  matrix products  33.6 us (15%)
  starting transfers between devices  16.5 us (7%)
  other arithmetic  14.4 us (6%)
  waiting for transfers between devices  3.45 us (2%)
    pallas_call x1, Pallas kernels, reduce_all(): pl.pallas_call(functools.partial(reduce_kernel, dims, count), name='reduc...  53.8 us
    pallas_call x1, Pallas kernels, gather_all(): pl.pallas_call(functools.partial(gather_kernel, dims, count), name='gathe...  48.7 us
    reshape x8, local copies, waits for them, and re-layouts, split_heads(): return values.reshape(image_count, window, head_count, head_width)  10.3 us
    ppermute x8, starting transfers between devices, shifted(): lax.ppermute(array, axis, [(i, (i + by) % length) for i in range(length)])  9.3 us
    dot_general x4, matrix products, dot_tail(): lax.dot_general(former, latter, (((1,), (1,)), ((), ())), preferred_eleme...  9.27 us
    unnamed x136, local copies, waits for them, and re-layouts  8.4 us
    dot_general x4, matrix products, dot_lead(): lax.dot_general(former, latter, (((0,), (0,)), ((), ())), preferred_eleme...  7.32 us
    ppermute x4, starting transfers between devices, shifted_both(): return lax.ppermute(array, ('rows', 'cols'), pairs)  7.24 us
  transfers between devices with their start and end apart: 12, of which 1 were waited for; matrix products, arithmetic and copies ran while one was open for 23% of the time, Pallas kernels for 46%

profile of v2, /device:TPU:0, one launch (start us, length us, event | category | flops | bytes accessed | tf_op | source)
XLA Modules:
  0.0 222.4 jit_solution(8008491815209820331)
XLA Ops:
  1.6 6.4 %collective-permute-start.8 = (f32[4,3,3,512]{3,0,2,1:T(4,128)S(1)}, f32[4,3,3,512]{3,0,2,1:T(4,128)S(1)}, u32[]{:S(2)}, u32[]{:S(2)}) collective-permute-start(f32[4,3,3,512]{3,0,2,1:T(4,128)S(1)} %slice.141), channel_id=1, source_target_pairs={{0,31},{1,28},{2,29},{3,30},{4,3},{5,0},{6,1},{7,2},{8,7},{9,4},{1... | collective-permute-start | bytes 221192 | tf_op jit(solution)/shard_map/ppermute | solution.py:73
  9.6 1.5 slice.140
  14.0 2.1 slice_reduce_fusion
  16.2 1.5 fusion.30.refs_4_
  17.6 48.7 %gather_all.1 = (bf16[2,2,2,4,16,1536]{5,4,3,2,1,0:T(8,128)(2,1)}, bf16[2,2,2,4,64,512]{5,4,3,2,1,0:T(8,128)(2,1)}, bf16[2,2,2,4,16,2048]{5,4,3,2,1,0:T(8,128)(2...) custom-call(bf16[16,1536]{1,0:T(8,128)(2,1)} %refs_0_.1, bf16[64,512]{1,0:T(8,128)(2,1)} %refs_1_.1, ...), custom_call_target="tpu_custom_call" | custom-call | bytes 150000000 | tf_op jit(solution)/shard_map/gather_all/pallas_call | solution.py:388
  67.8 1.2 convolution_bitcast_fusion
  69.7 1.5 slice.139
  75.2 4.0 %collective-permute-start.6 = (f32[4,4,3,512]{3,0,2,1:T(4,128)}, f32[4,4,3,512]{3,0,2,1:T(4,128)}, u32[]{:S(2)}, u32[]{:S(2)}) collective-permute-start(f32[4,4,3,512]{3,0,2,1:T(4,128)} %slice.139), channel_id=1, source_target_pairs={{0,3},{1,0},{2,1},{3,2},{4,7},{5,4},{6,5},{7,6},{8,11},{9,8},{10,9... | collective-permute-start | bytes 294920 | tf_op jit(solution)/shard_map/ppermute | solution.py:23
  81.1 1.0 add_convert_fusion.2
  83.3 1.5 copy.89
  85.3 1.6 copy.90
  88.1 2.1 fusion.41
  91.3 1.2 copy.94
  92.5 1.4 convert_element_type.254
  93.9 1.5 fusion.42
  95.7 3.8 %multiply_convert_fusion = (bf16[196,2048]{1,0:T(8,128)(2,1)S(1)}, f32[196,2048]{1,0:T(8,128)}) fusion(f32[2048]{0:T(1024)S(1)} %reshape.506, bf16[512,2048]{1,0:T(8,128)(2,1)} %bitcast.72, f32[196,512]{1,0:T(8,128)S(1)} %get-tuple-element.117, f32[512]{0:T(512)S(1)} %copy-done.43, f32[512]{0:T(512)S(1)} %reshape.504, f32[196]{0:T(256)S(1)} %add_rsqrt_fusion.1, ...), kind=kOutput, calls=%fused_computation.18 | convolution fusion | flops 413952000 | bytes 4920864 | tf_op jit(solution)/shard_map/dot_general | solution.py:45
  99.5 0.9 copy-done.6
  100.4 1.4 fusion.11
  102.7 1.1 reshape.476
  105.8 1.2 fusion.36
  107.7 1.7 convert_element_type.271
  110.3 1.1 reshape.477
  111.4 3.9 %fusion.43 = (f32[2048]{0:T(1024)}, bf16[196,2048]{1,0:T(8,128)(2,1)S(1)}) fusion(f32[196,2048]{1,0:T(8,128)} %get-tuple-element.122, bf16[196,512]{1,0:T(8,128)(2,1)} %convert_element_type.271, bf16[2048,512]{1,0:T(8,128)(2,1)} %bitcast.86), kind=kOutput, calls=%fused_computation.120 | convolution fusion | flops 415455232 | bytes 4714496 | tf_op jit(solution)/shard_map/dot_general | solution.py:55
  115.4 1.5 multiply_reduce_fusion.1
  116.9 1.5 fusion.34
  118.4 1.0 convolution_convert_fusion.6
  119.4 1.1 convolution_convert_fusion.3
  120.5 2.5 %reshape.511 = bf16[4,49,16,32]{3,2,1,0:T(8,128)(2,1)} reshape(bf16[196,512]{1,0:T(8,128)(2,1)} %convolution_convert_fusion.6) | data formatting | bytes 401408 | tf_op jit(solution)/shard_map/reshape | solution.py:553
  123.0 2.6 %copy.99 = bf16[4,49,16,32]{1,3,2,0:T(8,128)(2,1)} copy(bf16[4,49,16,32]{3,2,1,0:T(8,128)(2,1)} %reshape.511) | data formatting | bytes 401408 | tf_op jit(solution)/shard_map/reshape | solution.py:553
  125.6 2.5 %fusion.38 = (f32[16,32]{1,0:T(8,128)S(1)}, bf16[4,49,16,32]{1,3,2,0:T(8,128)(2,1)}) fusion(bf16[4,49,16,32]{1,3,2,0:T(8,128)(2,1)} %copy.99, f32[4,16,49,49]{2,3,1,0:T(8,128)S(1)} %get-tuple-element.115, f32[4,16,49]{2,1,0:T(8,128)S(1)} %copy-done.17), kind=kOutput, calls=%fused_computation.115 | convolution fusion | flops 10342016 | bytes 1030656 | tf_op jit(solution)/shard_map/whqk,wqhd->wkhd/dot_general | solution.py:615
  128.9 1.4 fusion.35
  130.3 1.4 fusion.8
  133.2 1.5 copy.106
  135.8 2.9 %multiply_reduce_fusion.2 = (f32[512]{0:T(512)S(1)}, f32[196]{0:T(256)S(1)}, f32[196]{0:T(256)S(1)}, f32[512]{0:T(512)S(1)}, f32[196,512]{1,0:T(8,128)}) fusion(f32[196,512]{1,0:T(8,128)S(1)} %reshape.467, f32[196]{0:T(256)S(1)} %div.33, f32[196]{0:T(256)S(1)} %rsqrt.22, f32[512]{0:T(512)S(1)} %copy-done.34, ...), kind=kOutput, calls=%fused_computation.47 | convolution fusion | flops 309183104 | bytes 2987072 | tf_op jit(solution)/shard_map/dot_general | solution.py:55
  138.7 1.9 convolution_convert_fusion.2
  140.7 2.2 convolution_convert_fusion
  143.0 2.1 convolution_convert_fusion.1
  145.0 1.0 reduce_sum.234
  147.6 1.7 collective-permute-start.5
  152.9 53.8 %reduce_all.1 = (f32[64,512]{1,0:T(8,128)}, f32[16,2048]{1,0:T(8,128)}, f32[16,1536]{1,0:T(8,128)}, f32[16,512]{1,0:T(8,128)}, f32[16,128]{1,0:T(8,128)}, /*index=5*/f32[24,128]{1,0:T(8,128)}) custom-call(bf16[2,2,2,4,64,512]{5,4,3,2,1,0:T(8,128)(2,1)} %bitcast.70, bf16[2,2,2,4,16,2048]{5,4,3,2,1,0:T(8,128)(2,1)} %bitcast.69, ...), custom_call_target="tpu_custom_call" | custom-call | bytes 150000000 | tf_op jit(solution)/shard_map/reduce_all/pallas_call | solution.py:436
  206.7 1.6 fusion.40
  208.3 1.0 slice.172
  209.5 1.3 slice.184
  210.8 0.9 collective-permute-start.10
  212.6 1.4 collective-permute-start.11
  214.2 1.0 copy.113
  215.2 3.4 %collective-permute-done.11 = bf16[4,4,3,512]{3,2,1,0:T(4,128)(2,1)S(1)} collective-permute-done((bf16[4,4,3,512]{3,2,1,0:T(4,128)(2,1)S(1)}, bf16[4,4,3,512]{3,2,1,0:T(4,128)(2,1)S(1)}, u32[]{:S(2)}, u32[]{:S(2)}) %collective-permute-start.11) | collective-permute-done | bytes 49184 | tf_op jit(solution)/shard_map/ppermute | solution.py:23
  218.8 1.0 copy.114
  (251 shorter events, 34.3 us)
Async XLA Ops:
  0.6 67.1 %copy-start = (f32[169,16]{0,1:T(8,128)S(1)}, f32[169,16]{0,1:T(8,128)}, u32[]{:S(2)}) copy-start(f32[169,16]{0,1:T(8,128)} %param.20) | copy-start | bytes 32452
  0.7 67.0 %copy-start.38 = (s32[49,49]{1,0:T(8,128)S(1)}, s32[49,49]{1,0:T(8,128)}, u32[]{:S(2)}) copy-start(s32[49,49]{1,0:T(8,128)} %param.19) | copy-start | bytes 28816
  1.6 73.6 %collective-permute-start.8 = (f32[4,3,3,512]{3,0,2,1:T(4,128)S(1)}, f32[4,3,3,512]{3,0,2,1:T(4,128)S(1)}, u32[]{:S(2)}, u32[]{:S(2)}) collective-permute-start(f32[4,3,3,512]{3,0,2,1:T(4,128)S(1)} %slice.141), channel_id=1, source_target_pairs={{0,31},{1,28},{2,29},{3,30},{4,3},{5,0},{6,1},{7,2},{8,7},{9,4},{1... | collective-permute-start | bytes 221192 | tf_op jit(solution)/shard_map/ppermute | solution.py:73
  8.9 70.9 %collective-permute-start.2 = (f32[4,3,3,512]{3,0,2,1:T(4,128)S(1)}, f32[4,3,3,512]{3,0,2,1:T(4,128)S(1)}, u32[]{:S(2)}, u32[]{:S(2)}) collective-permute-start(f32[4,3,3,512]{3,0,2,1:T(4,128)S(1)} %slice.121), channel_id=1, source_target_pairs={{0,31},{1,28},{2,29},{3,30},{4,3},{5,0},{6,1},{7,2},{8,7},{9,4},{1... | collective-permute-start | bytes 221192 | tf_op jit(solution)/shard_map/ppermute | solution.py:73
  11.1 94.7 %collective-permute-start.7 = (f32[4,3,4,512]{3,0,2,1:T(4,128)}, f32[4,3,4,512]{3,0,2,1:T(4,128)}, u32[]{:S(2)}, u32[]{:S(2)}) collective-permute-start(f32[4,3,4,512]{3,0,2,1:T(4,128)} %slice.140), channel_id=1, source_target_pairs={{0,28},{4,0},{8,4},{12,8},{16,12},{20,16},{24,20},{28,24},{1,29},{... | collective-permute-start | bytes 294920 | tf_op jit(solution)/shard_map/ppermute | solution.py:23
  12.2 67.6 %collective-permute-start.1 = (f32[4,3,4,512]{3,0,2,1:T(4,128)S(1)}, f32[4,3,4,512]{3,0,2,1:T(4,128)S(1)}, u32[]{:S(2)}, u32[]{:S(2)}) collective-permute-start(f32[4,3,4,512]{3,0,2,1:T(4,128)S(1)} %slice.120), channel_id=1, source_target_pairs={{0,28},{4,0},{8,4},{12,8},{16,12},{20,16},{24,20},{28,24},{1,29},{... | collective-permute-start | bytes 294920 | tf_op jit(solution)/shard_map/ppermute | solution.py:23
  13.6 66.2 %collective-permute-start = (f32[4,4,3,512]{3,0,2,1:T(4,128)S(1)}, f32[4,4,3,512]{3,0,2,1:T(4,128)S(1)}, u32[]{:S(2)}, u32[]{:S(2)}) collective-permute-start(f32[4,4,3,512]{3,0,2,1:T(4,128)S(1)} %slice.119), channel_id=1, source_target_pairs={{0,3},{1,0},{2,1},{3,2},{4,7},{5,4},{6,5},{7,6},{8,11},{9,8},{10,9... | collective-permute-start | bytes 294920 | tf_op jit(solution)/shard_map/ppermute | solution.py:23
  73.5 22.2 %copy-start.35 = (f32[512]{0:T(512)}, f32[512]{0:T(512)S(1)}, u32[]{:S(2)}) copy-start(f32[512]{0:T(512)S(1)} %reshape.504) | copy-start | bytes 6148
  73.6 8.5 %copy-start.33 = (f32[512]{0:T(512)}, f32[512]{0:T(512)S(1)}, u32[]{:S(2)}) copy-start(f32[512]{0:T(512)S(1)} %reshape.499) | copy-start | bytes 6148
  74.3 7.7 %copy-start.41 = (f32[512]{0:T(512)}, f32[512]{0:T(512)S(1)}, u32[]{:S(2)}) copy-start(f32[512]{0:T(512)S(1)} %reshape.500) | copy-start | bytes 6148
  75.1 4.6 %copy-start.23 = (f32[4,3,3,512]{3,0,2,1:T(4,128)}, f32[4,3,3,512]{3,0,2,1:T(4,128)S(1)}, u32[]{:S(2)}) copy-start(f32[4,3,3,512]{3,0,2,1:T(4,128)S(1)} %collective-permute-done.8) | copy-start | bytes 221188
  75.2 30.7 %collective-permute-start.6 = (f32[4,4,3,512]{3,0,2,1:T(4,128)}, f32[4,4,3,512]{3,0,2,1:T(4,128)}, u32[]{:S(2)}, u32[]{:S(2)}) collective-permute-start(f32[4,4,3,512]{3,0,2,1:T(4,128)} %slice.139), channel_id=1, source_target_pairs={{0,3},{1,0},{2,1},{3,2},{4,7},{5,4},{6,5},{7,6},{8,11},{9,8},{10,9... | collective-permute-start | bytes 294920 | tf_op jit(solution)/shard_map/ppermute | solution.py:23
  91.3 4.4 %copy-start.43 = (f32[512]{0:T(512)S(1)}, f32[512]{0:T(512)}, u32[]{:S(2)}) copy-start(f32[512]{0:T(512)} %reshape.505) | copy-start | bytes 6148
  93.9 5.6 %copy-start.9 = (bf16[196,512]{0,1:T(8,128)(2,1)}, bf16[196,512]{0,1:T(8,128)(2,1)S(1)}, u32[]{:S(2)}) copy-start(bf16[196,512]{0,1:T(8,128)(2,1)S(1)} %convert_element_type.254) | copy-start | bytes 602116
  95.4 19.9 %copy-start.39 = (f32[196]{0:T(256)}, f32[196]{0:T(256)S(1)}, u32[]{:S(2)}) copy-start(f32[196]{0:T(256)S(1)} %broadcast_multiply_fusion.5) | copy-start | bytes 2356
  95.7 3.8 %copy-start.45 = (f32[196]{0:T(256)}, f32[196]{0:T(256)S(1)}, u32[]{:S(2)}) copy-start(f32[196]{0:T(256)S(1)} %add_rsqrt_fusion.1) | copy-start | bytes 2356
  95.7 4.7 %copy-start.58 = (f32[512]{0:T(512)S(1)}, f32[512]{0:T(512)}, u32[]{:S(2)}) copy-start(f32[512]{0:T(512)} %reshape.507) | copy-start | bytes 6148
  95.7 4.7 %copy-start.61 = (bf16[2,2,2,4,64,512]{5,4,3,2,1,0:T(8,128)(2,1)S(1)}, bf16[2,2,2,4,64,512]{5,4,3,2,1,0:T(8,128)(2,1)}, u32[]{:S(2)}) copy-start(bf16[2,2,2,4,64,512]{5,4,3,2,1,0:T(8,128)(2,1)} %get-tuple-element.33) | copy-start | bytes 6291460
  103.7 5.7 %copy-start.8 = (f32[4,7,7,512]{3,2,1,0:T(8,128)}, f32[4,7,7,512]{3,2,1,0:T(8,128)S(1)}, u32[]{:S(2)}) copy-start(f32[4,7,7,512]{3,2,1,0:T(8,128)S(1)} %reshape.476) | copy-start | bytes 1204228
  111.4 4.0 %copy-start.11 = (bf16[2,2,2,4,16,2048]{5,4,3,2,1,0:T(8,128)(2,1)S(1)}, bf16[2,2,2,4,16,2048]{5,4,3,2,1,0:T(8,128)(2,1)}, u32[]{:S(2)}) copy-start(bf16[2,2,2,4,16,2048]{5,4,3,2,1,0:T(8,128)(2,1)} %get-tuple-element.32) | copy-start | bytes 6291460
  111.4 3.9 %copy-start.36 = (f32[512]{0:T(512)S(1)}, f32[512]{0:T(512)}, u32[]{:S(2)}) copy-start(f32[512]{0:T(512)} %copy-done.35) | copy-start | bytes 6148
  111.4 3.9 %copy-start.46 = (f32[196]{0:T(256)S(1)}, f32[196]{0:T(256)}, u32[]{:S(2)}) copy-start(f32[196]{0:T(256)} %copy-done.45) | copy-start | bytes 2356
  119.4 6.2 %copy-start.17 = (f32[4,16,49]{2,1,0:T(8,128)S(1)}, f32[4,16,49]{2,1,0:T(8,128)}, u32[]{:S(2)}) copy-start(f32[4,16,49]{2,1,0:T(8,128)} %copy-done.16) | copy-start | bytes 37636
  132.3 6.3 %copy-start.51 = (f32[196]{0:T(256)}, f32[196]{0:T(256)S(1)}, u32[]{:S(2)}) copy-start(f32[196]{0:T(256)S(1)} %div.33) | copy-start | bytes 2356
  142.9 4.1 %copy-start.53 = (f32[512]{0:T(512)S(1)}, f32[512]{0:T(512)}, u32[]{:S(2)}) copy-start(f32[512]{0:T(512)} %get-tuple-element.96) | copy-start | bytes 6148
  142.9 4.1 %copy-start.57 = (f32[512]{0:T(512)S(1)}, f32[512]{0:T(512)}, u32[]{:S(2)}) copy-start(f32[512]{0:T(512)} %reduce_sum.235) | copy-start | bytes 6148
  142.9 4.2 %copy-start.56 = (f32[2048]{0:T(1024)S(1)}, f32[2048]{0:T(1024)}, u32[]{:S(2)}) copy-start(f32[2048]{0:T(1024)} %get-tuple-element.126) | copy-start | bytes 24580
  142.9 4.2 %copy-start.54 = (f32[512]{0:T(512)S(1)}, f32[512]{0:T(512)}, u32[]{:S(2)}) copy-start(f32[512]{0:T(512)} %get-tuple-element.82) | copy-start | bytes 6148
  142.9 4.3 %copy-start.60 = (f32[512]{0:T(512)S(1)}, f32[512]{0:T(512)}, u32[]{:S(2)}) copy-start(f32[512]{0:T(512)} %get-tuple-element.74) | copy-start | bytes 6148
  142.9 4.4 %copy-start.59 = (f32[512]{0:T(512)S(1)}, f32[512]{0:T(512)}, u32[]{:S(2)}) copy-start(f32[512]{0:T(512)} %get-tuple-element.80) | copy-start | bytes 6148
  142.9 4.5 %copy-start.31 = (bf16[4,3,3,512]{3,2,1,0:T(4,128)(2,1)S(1)}, bf16[4,3,3,512]{3,2,1,0:T(4,128)(2,1)}, u32[]{:S(2)}) copy-start(bf16[4,3,3,512]{3,2,1,0:T(4,128)(2,1)} %slice.169) | copy-start | bytes 110596
  142.9 4.5 %copy-start.30 = (bf16[4,3,4,512]{3,2,1,0:T(4,128)(2,1)S(1)}, bf16[4,3,4,512]{3,2,1,0:T(4,128)(2,1)}, u32[]{:S(2)}) copy-start(bf16[4,3,4,512]{3,2,1,0:T(4,128)(2,1)} %slice.170) | copy-start | bytes 147460
  142.9 4.7 %copy-start.28 = (bf16[4,4,3,512]{3,2,1,0:T(4,128)(2,1)S(1)}, bf16[4,4,3,512]{3,2,1,0:T(4,128)(2,1)}, u32[]{:S(2)}) copy-start(bf16[4,4,3,512]{3,2,1,0:T(4,128)(2,1)} %slice.171) | copy-start | bytes 147460
  142.9 6.4 %copy-start.14 = (f32[16,49,49]{1,2,0:T(8,128)S(1)}, f32[16,49,49]{1,2,0:T(8,128)}, u32[]{:S(2)}) copy-start(f32[16,49,49]{1,2,0:T(8,128)} %get-tuple-element.84) | copy-start | bytes 460996
  143.0 6.8 %copy-start.50 = (s32[2401]{0:T(1024)S(1)}, s32[2401]{0:T(1024)}, u32[]{:S(2)}) copy-start(s32[2401]{0:T(1024)} %copy-done.49) | copy-start | bytes 28816
  145.0 5.8 %copy-start.22 = (f32[196,512]{1,0:T(8,128)S(1)}, f32[196,512]{1,0:T(8,128)}, u32[]{:S(2)}) copy-start(f32[196,512]{1,0:T(8,128)} %get-tuple-element.125) | copy-start | bytes 1204228
  145.0 5.8 %copy-start.52 = (f32[196]{0:T(256)S(1)}, f32[196]{0:T(256)}, u32[]{:S(2)}) copy-start(f32[196]{0:T(256)} %copy-done.51) | copy-start | bytes 2356
  147.4 66.6 %collective-permute-start.3 = (bf16[4,3,3,512]{3,2,1,0:T(4,128)(2,1)S(1)}, bf16[4,3,3,512]{3,2,1,0:T(4,128)(2,1)S(1)}, u32[]{:S(2)}, u32[]{:S(2)}) collective-permute-start(bf16[4,3,3,512]{3,2,1,0:T(4,128)(2,1)S(1)} %copy-done.31), channel_id=1, source_target_pairs={{0,5},{1,6},{2,7},{3,4},{4,9},{5,10},{6,11},{7,8},{8,13},{9,14},{1... | collective-permute-start | bytes 110600 | tf_op jit(solution)/shard_map/ppermute | solution.py:73
  147.4 66.6 %collective-permute-start.4 = (bf16[4,3,4,512]{3,2,1,0:T(4,128)(2,1)S(1)}, bf16[4,3,4,512]{3,2,1,0:T(4,128)(2,1)S(1)}, u32[]{:S(2)}, u32[]{:S(2)}) collective-permute-start(bf16[4,3,4,512]{3,2,1,0:T(4,128)(2,1)S(1)} %copy-done.30), channel_id=1, source_target_pairs={{0,4},{4,8},{8,12},{12,16},{16,20},{20,24},{24,28},{28,0},{1,5},{5... | collective-permute-start | bytes 147464 | tf_op jit(solution)/shard_map/ppermute | solution.py:23
  147.6 65.0 %collective-permute-start.5 = (bf16[4,4,3,512]{3,2,1,0:T(4,128)(2,1)S(1)}, bf16[4,4,3,512]{3,2,1,0:T(4,128)(2,1)S(1)}, u32[]{:S(2)}, u32[]{:S(2)}) collective-permute-start(bf16[4,4,3,512]{3,2,1,0:T(4,128)(2,1)S(1)} %copy-done.28), channel_id=1, source_target_pairs={{0,1},{1,2},{2,3},{3,0},{4,5},{5,6},{6,7},{7,4},{8,9},{9,10},{10,1... | collective-permute-start | bytes 147464 | tf_op jit(solution)/shard_map/ppermute | solution.py:23
  206.7 5.1 %copy-start.48 = (f32[24,128]{1,0:T(8,128)S(1)}, f32[24,128]{1,0:T(8,128)}, u32[]{:S(2)}) copy-start(f32[24,128]{1,0:T(8,128)} %get-tuple-element.41) | copy-start | bytes 36868
  210.7 7.9 %collective-permute-start.9 = (bf16[4,3,3,512]{3,2,1,0:T(4,128)(2,1)S(1)}, bf16[4,3,3,512]{3,2,1,0:T(4,128)(2,1)S(1)}, u32[]{:S(2)}, u32[]{:S(2)}) collective-permute-start(bf16[4,3,3,512]{3,2,1,0:T(4,128)(2,1)S(1)} %slice.173), channel_id=1, source_target_pairs={{0,5},{1,6},{2,7},{3,4},{4,9},{5,10},{6,11},{7,8},{8,13},{9,14},{1... | collective-permute-start | bytes 110600 | tf_op jit(solution)/shard_map/ppermute | solution.py:73
  210.8 7.8 %collective-permute-start.10 = (bf16[4,3,4,512]{3,2,1,0:T(4,128)(2,1)S(1)}, bf16[4,3,4,512]{3,2,1,0:T(4,128)(2,1)S(1)}, u32[]{:S(2)}, u32[]{:S(2)}) collective-permute-start(bf16[4,3,4,512]{3,2,1,0:T(4,128)(2,1)S(1)} %slice.174), channel_id=1, source_target_pairs={{0,4},{4,8},{8,12},{12,16},{16,20},{20,24},{24,28},{28,0},{1,5},{5... | collective-permute-start | bytes 147464 | tf_op jit(solution)/shard_map/ppermute | solution.py:23
  212.6 6.1 %collective-permute-start.11 = (bf16[4,4,3,512]{3,2,1,0:T(4,128)(2,1)S(1)}, bf16[4,4,3,512]{3,2,1,0:T(4,128)(2,1)S(1)}, u32[]{:S(2)}, u32[]{:S(2)}) collective-permute-start(bf16[4,4,3,512]{3,2,1,0:T(4,128)(2,1)S(1)} %slice.175), channel_id=1, source_target_pairs={{0,1},{1,2},{2,3},{3,0},{4,5},{5,6},{6,7},{7,4},{8,9},{9,10},{10,1... | collective-permute-start | bytes 147464 | tf_op jit(solution)/shard_map/ppermute | solution.py:23
  214.1 5.7 %copy-start.27 = (f32[16,1536]{1,0:T(8,128)S(1)}, f32[16,1536]{1,0:T(8,128)}, u32[]{:S(2)}) copy-start(f32[16,1536]{1,0:T(8,128)} %get-tuple-element.152) | copy-start | bytes 294916
  214.2 6.3 %copy-start.32 = (f32[16,512]{1,0:T(8,128)S(1)}, f32[16,512]{1,0:T(8,128)}, u32[]{:S(2)}) copy-start(f32[16,512]{1,0:T(8,128)} %get-tuple-element.153) | copy-start | bytes 98308
  214.2 6.9 %copy-start.26 = (f32[16,2048]{1,0:T(8,128)S(1)}, f32[16,2048]{1,0:T(8,128)}, u32[]{:S(2)}) copy-start(f32[16,2048]{1,0:T(8,128)} %get-tuple-element.154) | copy-start | bytes 393220
  214.2 7.6 %copy-start.25 = (f32[64,512]{1,0:T(8,128)S(1)}, f32[64,512]{1,0:T(8,128)}, u32[]{:S(2)}) copy-start(f32[64,512]{1,0:T(8,128)} %get-tuple-element.155) | copy-start | bytes 393220
  (26 other events, 50.4 us)
